TPU v7x, 512 devices: a whole 4x8x8 slice. The times are simulated.
512 devices in a mesh: rows: 128 (over y, z, core), feat: 4 (over x).
Axes of the slice: x: 4, y: 8, z: 8, core: 2. Of those that a mesh axis runs over, the one named last changes fastest.
Arguments:
- features: bfloat16 [1048576, 1024], P('rows', 'feat'), may hold values from -6 to 6
- gradients: float32 [1048576], P(('rows', 'feat')), may hold values from -2.7 to 2.7
- hessians: float32 [1048576], P(('rows', 'feat')), may hold values from 0.05 to 0.75
- node_ids: int32 [1048576], P('rows'), may hold values from 0 to 3
- sample_flags: int32 [1048576], P('rows'), may hold values 0 or 1
- kept_index: int32 [524288], P('rows'), may hold values from 0 to 8191, as said below
- kept_count: int32 [128], P('rows'), may hold values from 1 to 4096, 131072 in all
- cut_edges: int32 [1024, 128], P('feat'), may hold values from 0 to 128
Outputs:
- split_gain: float32 [1024, 4, 128], P(('feat', 'rows'))
- cut_rank: float32 [1024, 4, 128], P(('feat', 'rows'))
Inputs may be any that keep to these rules, and one draw needn't show every extreme that they name: `kept_index`: within the 4096 entries of one index of rows the numbers are distinct local row numbers; entries at slot kept_count of that index or later are not used. `kept_count`: one count for each index of rows; the counts sum to exactly 131072, and the largest is exactly 4096.
All inputs are finite; a program needn't handle non-finite values. No bound on the sum of `sample_flags` on one device may be relied on, other than what follows from the above.
Results may differ from a plain program's by a relative error of at most 0.007.
Values may be sent and summed in bfloat16 or wider, within the bound.
A program may use at most 64 MiB of HBM per device.

v0:
```python
import math

import jax
import jax.numpy as jnp
from jax import lax
from jax.sharding import PartitionSpec as P

NODES = 4


amplify_factor = 8.0
regularize = 1.0
edge_step = 0.0625
edge_anchor = 4.0


def histogram(kept_columns, kept_weights, cut_values):
    feature_count, slot_count = kept_columns.shape
    feature_width = math.gcd(feature_count, 16)
    slot_width = math.gcd(slot_count, 1024)
    weight_rows = kept_weights.shape[0]
    cut_count = cut_values.shape[1]

    def feature_block(i):
        block_rows = lax.dynamic_slice_in_dim(kept_columns, i * feature_width, feature_width, 0)
        block_cuts = lax.dynamic_slice_in_dim(cut_values, i * feature_width, feature_width, 0)

        def add_slots(j, running):
            slot_part = lax.dynamic_slice_in_dim(block_rows, j * slot_width, slot_width, 1)
            weight_part = lax.dynamic_slice_in_dim(kept_weights, j * slot_width, slot_width, 1)
            compare = (slot_part.astype(jnp.float32)[:, None, :] <= block_cuts[:, :, None]).astype(
                jnp.bfloat16
            )
            compare = compare.reshape(feature_width * cut_count, slot_width)
            return running + lax.dot_general(
                weight_part, compare, (((1,), (1,)), ((), ())), preferred_element_type=jnp.float32
            )

        start_value = jnp.zeros((weight_rows, feature_width * cut_count), jnp.float32)
        running = lax.fori_loop(0, slot_count // slot_width, add_slots, start_value)
        return running.reshape(weight_rows, feature_width, cut_count).transpose(1, 0, 2)

    blocks = lax.map(feature_block, jnp.arange(feature_count // feature_width, dtype=jnp.int32))
    return blocks.reshape(feature_count, weight_rows, cut_count)


def split_gains(node_hist, totals, node_count):
    grad_left = node_hist[:, :node_count]
    hess_left = node_hist[:, node_count:]
    grad_sum = totals[:node_count][None, :, None]
    hess_sum = totals[node_count:][None, :, None]
    split_gain = (
        grad_left * grad_left / (hess_left + regularize)
        + (grad_sum - grad_left) ** 2 / (hess_sum - hess_left + regularize)
        - grad_sum * grad_sum / (hess_sum + regularize)
    )
    cut_rank = hess_left / hess_sum
    return (split_gain, cut_rank)


def shards(
    features, gradients, hessians, node_ids, sample_flags, kept_index, kept_count, cut_edges
):
    grad_rows, hess_rows = (
        lax.all_gather(gradients, "feat", axis=0, tiled=True),
        lax.all_gather(hessians, "feat", axis=0, tiled=True),
    )
    slot_total = kept_index.shape[0]
    live_slot = jnp.arange(slot_total, dtype=jnp.int32) < kept_count[0]
    factor = jnp.where(sample_flags[kept_index] == 1, jnp.float32(amplify_factor), jnp.float32(1.0))
    grad_weight = jnp.where(live_slot, grad_rows[kept_index] * factor, 0.0).astype(jnp.bfloat16)
    hess_weight = jnp.where(live_slot, hess_rows[kept_index] * factor, 0.0).astype(jnp.bfloat16)
    node_of = node_ids[kept_index]
    onehot = jnp.arange(NODES, dtype=jnp.int32)[:, None] == node_of[None, :]
    zero_value = jnp.zeros((), jnp.bfloat16)
    kept_weights = jnp.concatenate(
        [
            jnp.where(onehot, grad_weight[None, :], zero_value),
            jnp.where(onehot, hess_weight[None, :], zero_value),
        ],
        axis=0,
    )
    kept_columns = features[kept_index].T
    cut_values = cut_edges.astype(jnp.float32) * edge_step - edge_anchor
    owned_count = cut_values.shape[0] // lax.axis_size("rows")
    whole_hist, totals = lax.psum(
        (
            histogram(kept_columns, kept_weights, cut_values),
            jnp.sum(kept_weights.astype(jnp.float32), axis=1),
        ),
        "rows",
    )
    node_hist = lax.dynamic_slice_in_dim(
        whole_hist, lax.axis_index("rows") * owned_count, owned_count, 0
    )
    return split_gains(node_hist, totals, NODES)


def solution(mesh):
    placed = (
        P("rows", "feat"),
        P(("rows", "feat")),
        P(("rows", "feat")),
        P("rows"),
        P("rows"),
        P("rows"),
        P("rows"),
        P("feat", None),
    )
    return jax.shard_map(
        shards,
        mesh=mesh,
        in_specs=placed,
        out_specs=(P(("feat", "rows"), None, None), P(("feat", "rows"), None, None)),
        check_vma=False,
    )
```

profile of v0, /device:TPU:1, one launch (start us, length us, event | category | flops | bytes accessed | tf_op | source)
XLA Modules:
  0.0 618.7 jit_solution(16730653097774385124)
XLA Ops:
  8.6 23.0 %gather_fusion.3 = s32[4096]{0:T(1024)S(1)} fusion(s32[8192]{0:T(1024)S(1)} %copy-done, s32[4096]{0:T(1024)S(1)} %fusion.8), kind=kCustom, calls=%fused_computation.3 | custom fusion | bytes 49152 | tf_op jit(solution)/shard_map/gather | solution.py:70
  31.7 23.0 %gather_fusion.1 = s32[4096]{0:T(1024)S(1)} fusion(s32[8192]{0:T(1024)S(1)} %copy-done.1, s32[4096]{0:T(1024)S(1)} %fusion.8), kind=kCustom, calls=%fused_computation.1 | custom fusion | bytes 49152 | tf_op jit(solution)/shard_map/gather | solution.py:73
  54.7 10.2 %all_gather.6 = f32[8192]{0:T(1024)S(1)} all-gather(f32[2048]{0:T(1024)S(1)} %copy-done.3), channel_id=1, replica_groups=mesh['rows'=128,'feat'=4] {'feat'}, dimensions={0}, use_global_device_ids=true | all-gather | bytes 40960 | tf_op jit(solution)/shard_map/all_gather | solution.py:65
  64.9 23.0 %gather_fusion.2 = f32[4096]{0:T(1024)S(1)} fusion(f32[8192]{0:T(1024)S(1)} %all_gather.6, s32[4096]{0:T(1024)S(1)} %fusion.8), kind=kCustom, calls=%fused_computation.2 | custom fusion | bytes 49152 | tf_op jit(solution)/shard_map/gather | solution.py:71
  88.0 9.0 %all_gather.7 = f32[8192]{0:T(1024)S(1)} all-gather(f32[2048]{0:T(1024)S(1)} %copy-done.4), channel_id=1, replica_groups=mesh['rows'=128,'feat'=4] {'feat'}, dimensions={0}, use_global_device_ids=true | all-gather | bytes 40960 | tf_op jit(solution)/shard_map/all_gather | solution.py:66
  97.0 23.0 %gather_fusion.4 = f32[4096]{0:T(1024)S(1)} fusion(f32[8192]{0:T(1024)S(1)} %all_gather.7, s32[4096]{0:T(1024)S(1)} %fusion.8), kind=kCustom, calls=%fused_computation.4 | custom fusion | bytes 49152 | tf_op jit(solution)/shard_map/gather | solution.py:72
  120.1 15.7 %gather_fusion = bf16[4096,256]{1,0:T(8,128)(2,1)S(1)} fusion(bf16[8192,256]{1,0:T(8,128)(2,1)} %param.12, s32[4096]{0:T(1024)S(1)} %fusion.8), kind=kCustom, calls=%fused_computation | custom fusion | bytes 4210688 | tf_op jit(solution)/shard_map/gather | solution.py:83
  135.8 2.9 copy.12
  138.9 211.5 %while.25 = (s32[]{:T(128)}, f32[16,16,8,128]{3,2,1,0:T(8,128)}, s32[16]{0:T(128)S(1)}, bf16[256,4096]{1,0:T(8,128)(2,1)}, f32[256,128]{1,0:T(8,128)S(1)}, /*ind...) while((s32[]{:T(128)}, f32[16,16,8,128]{3,2,1,0:T(8,128)}, ...), condition=%wide.region_3.4_spmd, body=%wide.region_0.3_spmd.sunk | while | flops 35700748 | bytes 4923848 | solution.py:43
  141.2 10.3 %while.26 = (s32[]{:T(128)}, f32[8,2048]{1,0:T(8,128)S(1)}, bf16[8,4096]{1,0:T(8,128)(2,1)S(1)}, bf16[16,4096]{1,0:T(8,128)(2,1)S(1)}, f32[16,128]{1,0:T(8,128)S...) while((s32[]{:T(128)}, f32[8,2048]{1,0:T(8,128)S(1)}, bf16[8,4096]{1,0:T(8,128)(2,1)S(1)}, ...), condition=%wide.region_2.2_spmd.clone, body=%wide.region_1.1_spmd.clone.sunk | while | flops 35700744 | bytes 4513957 | solution.py:40
  141.2 1.3 bitcast_compare_fusion.2
  143.8 1.3 bitcast_compare_fusion.2
  146.4 1.3 bitcast_compare_fusion.2
  148.9 1.3 bitcast_compare_fusion.2
  154.4 10.3 %while.26 = (s32[]{:T(128)}, f32[8,2048]{1,0:T(8,128)S(1)}, bf16[8,4096]{1,0:T(8,128)(2,1)S(1)}, bf16[16,4096]{1,0:T(8,128)(2,1)S(1)}, f32[16,128]{1,0:T(8,128)S...) while((s32[]{:T(128)}, f32[8,2048]{1,0:T(8,128)S(1)}, bf16[8,4096]{1,0:T(8,128)(2,1)S(1)}, ...), condition=%wide.region_2.2_spmd.clone, body=%wide.region_1.1_spmd.clone.sunk | while | flops 35700744 | bytes 4513957 | solution.py:40
  154.4 1.3 bitcast_compare_fusion.2
  159.6 1.3 bitcast_compare_fusion.2
  162.1 1.3 bitcast_compare_fusion.2
  167.6 10.3 %while.26 = (s32[]{:T(128)}, f32[8,2048]{1,0:T(8,128)S(1)}, bf16[8,4096]{1,0:T(8,128)(2,1)S(1)}, bf16[16,4096]{1,0:T(8,128)(2,1)S(1)}, f32[16,128]{1,0:T(8,128)S...) while((s32[]{:T(128)}, f32[8,2048]{1,0:T(8,128)S(1)}, bf16[8,4096]{1,0:T(8,128)(2,1)S(1)}, ...), condition=%wide.region_2.2_spmd.clone, body=%wide.region_1.1_spmd.clone.sunk | while | flops 35700744 | bytes 4513957 | solution.py:40
  167.7 1.3 bitcast_compare_fusion.2
  172.8 1.3 bitcast_compare_fusion.2
  175.4 1.3 bitcast_compare_fusion.2
  180.8 10.3 %while.26 = (s32[]{:T(128)}, f32[8,2048]{1,0:T(8,128)S(1)}, bf16[8,4096]{1,0:T(8,128)(2,1)S(1)}, bf16[16,4096]{1,0:T(8,128)(2,1)S(1)}, f32[16,128]{1,0:T(8,128)S...) while((s32[]{:T(128)}, f32[8,2048]{1,0:T(8,128)S(1)}, bf16[8,4096]{1,0:T(8,128)(2,1)S(1)}, ...), condition=%wide.region_2.2_spmd.clone, body=%wide.region_1.1_spmd.clone.sunk | while | flops 35700744 | bytes 4513957 | solution.py:40
  180.9 1.3 bitcast_compare_fusion.2
  183.5 1.3 bitcast_compare_fusion.2
  186.0 1.3 bitcast_compare_fusion.2
  188.6 1.3 bitcast_compare_fusion.2
  194.1 10.3 %while.26 = (s32[]{:T(128)}, f32[8,2048]{1,0:T(8,128)S(1)}, bf16[8,4096]{1,0:T(8,128)(2,1)S(1)}, bf16[16,4096]{1,0:T(8,128)(2,1)S(1)}, f32[16,128]{1,0:T(8,128)S...) while((s32[]{:T(128)}, f32[8,2048]{1,0:T(8,128)S(1)}, bf16[8,4096]{1,0:T(8,128)(2,1)S(1)}, ...), condition=%wide.region_2.2_spmd.clone, body=%wide.region_1.1_spmd.clone.sunk | while | flops 35700744 | bytes 4513957 | solution.py:40
  194.1 1.3 bitcast_compare_fusion.2
  199.2 1.3 bitcast_compare_fusion.2
  201.8 1.3 bitcast_compare_fusion.2
  207.3 10.3 %while.26 = (s32[]{:T(128)}, f32[8,2048]{1,0:T(8,128)S(1)}, bf16[8,4096]{1,0:T(8,128)(2,1)S(1)}, bf16[16,4096]{1,0:T(8,128)(2,1)S(1)}, f32[16,128]{1,0:T(8,128)S...) while((s32[]{:T(128)}, f32[8,2048]{1,0:T(8,128)S(1)}, bf16[8,4096]{1,0:T(8,128)(2,1)S(1)}, ...), condition=%wide.region_2.2_spmd.clone, body=%wide.region_1.1_spmd.clone.sunk | while | flops 35700744 | bytes 4513957 | solution.py:40
  209.9 1.3 bitcast_compare_fusion.2
  215.0 1.3 bitcast_compare_fusion.2
  220.5 10.3 %while.26 = (s32[]{:T(128)}, f32[8,2048]{1,0:T(8,128)S(1)}, bf16[8,4096]{1,0:T(8,128)(2,1)S(1)}, bf16[16,4096]{1,0:T(8,128)(2,1)S(1)}, f32[16,128]{1,0:T(8,128)S...) while((s32[]{:T(128)}, f32[8,2048]{1,0:T(8,128)S(1)}, bf16[8,4096]{1,0:T(8,128)(2,1)S(1)}, ...), condition=%wide.region_2.2_spmd.clone, body=%wide.region_1.1_spmd.clone.sunk | while | flops 35700744 | bytes 4513957 | solution.py:40
  223.1 1.3 bitcast_compare_fusion.2
  225.7 1.3 bitcast_compare_fusion.2
  233.7 10.3 %while.26 = (s32[]{:T(128)}, f32[8,2048]{1,0:T(8,128)S(1)}, bf16[8,4096]{1,0:T(8,128)(2,1)S(1)}, bf16[16,4096]{1,0:T(8,128)(2,1)S(1)}, f32[16,128]{1,0:T(8,128)S...) while((s32[]{:T(128)}, f32[8,2048]{1,0:T(8,128)S(1)}, bf16[8,4096]{1,0:T(8,128)(2,1)S(1)}, ...), condition=%wide.region_2.2_spmd.clone, body=%wide.region_1.1_spmd.clone.sunk | while | flops 35700744 | bytes 4513957 | solution.py:40
  246.9 10.3 %while.26 = (s32[]{:T(128)}, f32[8,2048]{1,0:T(8,128)S(1)}, bf16[8,4096]{1,0:T(8,128)(2,1)S(1)}, bf16[16,4096]{1,0:T(8,128)(2,1)S(1)}, f32[16,128]{1,0:T(8,128)S...) while((s32[]{:T(128)}, f32[8,2048]{1,0:T(8,128)S(1)}, bf16[8,4096]{1,0:T(8,128)(2,1)S(1)}, ...), condition=%wide.region_2.2_spmd.clone, body=%wide.region_1.1_spmd.clone.sunk | while | flops 35700744 | bytes 4513957 | solution.py:40
  260.1 10.3 %while.26 = (s32[]{:T(128)}, f32[8,2048]{1,0:T(8,128)S(1)}, bf16[8,4096]{1,0:T(8,128)(2,1)S(1)}, bf16[16,4096]{1,0:T(8,128)(2,1)S(1)}, f32[16,128]{1,0:T(8,128)S...) while((s32[]{:T(128)}, f32[8,2048]{1,0:T(8,128)S(1)}, bf16[8,4096]{1,0:T(8,128)(2,1)S(1)}, ...), condition=%wide.region_2.2_spmd.clone, body=%wide.region_1.1_spmd.clone.sunk | while | flops 35700744 | bytes 4513957 | solution.py:40
  273.4 10.3 %while.26 = (s32[]{:T(128)}, f32[8,2048]{1,0:T(8,128)S(1)}, bf16[8,4096]{1,0:T(8,128)(2,1)S(1)}, bf16[16,4096]{1,0:T(8,128)(2,1)S(1)}, f32[16,128]{1,0:T(8,128)S...) while((s32[]{:T(128)}, f32[8,2048]{1,0:T(8,128)S(1)}, bf16[8,4096]{1,0:T(8,128)(2,1)S(1)}, ...), condition=%wide.region_2.2_spmd.clone, body=%wide.region_1.1_spmd.clone.sunk | while | flops 35700744 | bytes 4513957 | solution.py:40
  286.6 10.3 %while.26 = (s32[]{:T(128)}, f32[8,2048]{1,0:T(8,128)S(1)}, bf16[8,4096]{1,0:T(8,128)(2,1)S(1)}, bf16[16,4096]{1,0:T(8,128)(2,1)S(1)}, f32[16,128]{1,0:T(8,128)S...) while((s32[]{:T(128)}, f32[8,2048]{1,0:T(8,128)S(1)}, bf16[8,4096]{1,0:T(8,128)(2,1)S(1)}, ...), condition=%wide.region_2.2_spmd.clone, body=%wide.region_1.1_spmd.clone.sunk | while | flops 35700744 | bytes 4513957 | solution.py:40
  299.8 10.3 %while.26 = (s32[]{:T(128)}, f32[8,2048]{1,0:T(8,128)S(1)}, bf16[8,4096]{1,0:T(8,128)(2,1)S(1)}, bf16[16,4096]{1,0:T(8,128)(2,1)S(1)}, f32[16,128]{1,0:T(8,128)S...) while((s32[]{:T(128)}, f32[8,2048]{1,0:T(8,128)S(1)}, bf16[8,4096]{1,0:T(8,128)(2,1)S(1)}, ...), condition=%wide.region_2.2_spmd.clone, body=%wide.region_1.1_spmd.clone.sunk | while | flops 35700744 | bytes 4513957 | solution.py:40
  313.0 10.3 %while.26 = (s32[]{:T(128)}, f32[8,2048]{1,0:T(8,128)S(1)}, bf16[8,4096]{1,0:T(8,128)(2,1)S(1)}, bf16[16,4096]{1,0:T(8,128)(2,1)S(1)}, f32[16,128]{1,0:T(8,128)S...) while((s32[]{:T(128)}, f32[8,2048]{1,0:T(8,128)S(1)}, bf16[8,4096]{1,0:T(8,128)(2,1)S(1)}, ...), condition=%wide.region_2.2_spmd.clone, body=%wide.region_1.1_spmd.clone.sunk | while | flops 35700744 | bytes 4513957 | solution.py:40
  326.2 10.3 %while.26 = (s32[]{:T(128)}, f32[8,2048]{1,0:T(8,128)S(1)}, bf16[8,4096]{1,0:T(8,128)(2,1)S(1)}, bf16[16,4096]{1,0:T(8,128)(2,1)S(1)}, f32[16,128]{1,0:T(8,128)S...) while((s32[]{:T(128)}, f32[8,2048]{1,0:T(8,128)S(1)}, bf16[8,4096]{1,0:T(8,128)(2,1)S(1)}, ...), condition=%wide.region_2.2_spmd.clone, body=%wide.region_1.1_spmd.clone.sunk | while | flops 35700744 | bytes 4513957 | solution.py:40
  339.4 10.3 %while.26 = (s32[]{:T(128)}, f32[8,2048]{1,0:T(8,128)S(1)}, bf16[8,4096]{1,0:T(8,128)(2,1)S(1)}, bf16[16,4096]{1,0:T(8,128)(2,1)S(1)}, f32[16,128]{1,0:T(8,128)S...) while((s32[]{:T(128)}, f32[8,2048]{1,0:T(8,128)S(1)}, bf16[8,4096]{1,0:T(8,128)(2,1)S(1)}, ...), condition=%wide.region_2.2_spmd.clone, body=%wide.region_1.1_spmd.clone.sunk | while | flops 35700744 | bytes 4513957 | solution.py:40
  350.6 259.8 %psum.15 = f32[8]{0:T(128)S(1)} all-reduce(f32[8]{0:T(128)S(1)} %convert_reduce_fusion), channel_id=1, replica_groups=mesh['rows'=128,'feat'=4] {'rows'}, use_global_device_ids=true, to_apply=%region_6.7 | all-reduce | flops 8 | bytes 64 | tf_op jit(solution)/shard_map/psum | solution.py:86
  610.4 1.4 dynamic-slice_divide_fusion
  (274 shorter events, 171.7 us)
Async XLA Ops:
  7.2 1.4 copy-start
  7.2 603.2 %all-reduce.2.cloned.1.call-start = ((), (), s32[]{:S(2)}) async-start(), calls=%async_computation | async-start | bytes 2097152 | tf_op jit(solution)/shard_map/psum | solution.py:86
  8.6 23.1 %copy-start.1 = (s32[8192]{0:T(1024)S(1)}, s32[8192]{0:T(1024)}, u32[]{:S(2)}) copy-start(s32[8192]{0:T(1024)} %param.15) | copy-start | bytes 98308
  31.7 23.1 %copy-start.3 = (f32[2048]{0:T(1024)S(1)}, f32[2048]{0:T(1024)}, u32[]{:S(2)}) copy-start(f32[2048]{0:T(1024)} %param.13) | copy-start | bytes 24580
  64.9 23.0 %copy-start.4 = (f32[2048]{0:T(1024)S(1)}, f32[2048]{0:T(1024)}, u32[]{:S(2)}) copy-start(f32[2048]{0:T(1024)} %param.14) | copy-start | bytes 24580
  97.0 23.0 %copy-start.2 = (s32[256,128]{1,0:T(8,128)S(1)}, s32[256,128]{1,0:T(8,128)}, u32[]{:S(2)}) copy-start(s32[256,128]{1,0:T(8,128)} %param.19) | copy-start | bytes 393220
Sparse Core Ops, SparseCore 0:
  350.5 206.7 all-reduce.1
where the time goes:
time: 619 us
  blocking collectives  279 us (45%)
  local copies, waits for them, and re-layouts  146 us (24%)
  other arithmetic  89.7 us (14%)
  matrix products  76 us (12%)
  between operations  14.8 us (2%)
  loops' own time  12.7 us (2%)
    psum x1, blocking collectives, shards(): lax.psum((histogram(kept_columns, kept_weights, cut_values), jnp.sum(kept...  260 us
    le x64, other arithmetic, add_slots(): slot_part.astype(jnp.float32)[:, None, :] <= block_cuts[:, :, None]  86.2 us
    dot_general x64, matrix products, add_slots(): lax.dot_general(weight_part, compare, (((1,), (1,)), ((), ())), preferred...  76 us
    gather x1, local copies, waits for them, and re-layouts, shards(): sample_flags[kept_index] == 1  23 us
    gather x1, local copies, waits for them, and re-layouts, shards(): node_of = node_ids[kept_index]  23 us
    gather x1, local copies, waits for them, and re-layouts, shards(): grad_rows[kept_index] * factor  23 us
    gather x1, local copies, waits for them, and re-layouts, shards(): hess_rows[kept_index] * factor  23 us
    gather x1, local copies, waits for them, and re-layouts, shards(): kept_columns = features[kept_index].T  15.7 us
  transfers between devices with their start and end apart: 1, of which 0 were waited for; matrix products, arithmetic and copies ran while one was open for 0% of the time, Pallas kernels for 0%

commit v1 on v0

v1 whole, which is shorter than its diff:
```python
import functools

import jax
import jax.numpy as jnp
from jax import lax
from jax.experimental import pallas as pl
from jax.experimental.pallas import tpu as pltpu
from jax.sharding import PartitionSpec as P

MESH = pl.DeviceIdType.MESH
NODES = 4
BLOCK = 256
WIN = 64
NT = (((1,), (1,)), ((), ()))
VM = pl.BlockSpec(memory_space=pltpu.VMEM)
SM = pl.BlockSpec(memory_space=pltpu.SMEM)
HBM = pl.BlockSpec(memory_space=pl.ANY)
F32, BF16, I32 = jnp.float32, jnp.bfloat16, jnp.int32


def iota(shape, dim, kind=I32):
    return lax.broadcasted_iota(I32, shape, dim).astype(kind)


def onehot(cond):
    return jnp.where(cond, 1.0, 0.0).astype(BF16)


def share_body(peers, g_ref, h_ref, out_ref, send_sem, recv_sem):
    row, me = lax.axis_index("rows"), lax.axis_index("feat")
    barrier = pltpu.get_barrier_semaphore()
    for d in range(1, peers):
        pl.semaphore_signal(barrier, inc=1, device_id=(row, lax.rem(me + d, peers)), device_id_type=MESH)
    out_ref[me, 0] = g_ref[...]
    out_ref[me, 1] = h_ref[...]
    pl.semaphore_wait(barrier, peers - 1)
    copies = []
    for d in range(1, peers):
        to = (row, lax.rem(me + d, peers))
        for w, ref in enumerate((g_ref, h_ref)):
            copies.append(
                pltpu.make_async_remote_copy(
                    src_ref=ref,
                    dst_ref=out_ref.at[me, w],
                    send_sem=send_sem.at[d, w],
                    recv_sem=recv_sem.at[d, w],
                    device_id=to,
                    device_id_type=MESH,
                )
            )
    for c in copies:
        c.start()
    for c in copies:
        c.wait()


def share(gradients, hessians, peers):
    part = gradients.shape[0]
    return pl.pallas_call(
        functools.partial(share_body, peers),
        out_shape=jax.ShapeDtypeStruct((peers, 2, part // 128, 128), F32),
        in_specs=[VM, VM],
        out_specs=VM,
        scratch_shapes=[pltpu.SemaphoreType.DMA((peers, 2)), pltpu.SemaphoreType.DMA((peers, 2))],
        compiler_params=pltpu.CompilerParams(collective_id=0, has_side_effects=True),
        name="share",
    )(gradients.reshape(part // 128, 128), hessians.reshape(part // 128, 128))


def hist_body(
    cnt_s, feat, idx_v, gh, node_v, flag_v, main, extra,
    xb, xs, ws, pos, tpose, hi_s, lo_s, w16_s, acc, exacc, totacc, offs_v, offs_s, ext, sem, osem,
):
    rows, width = feat.shape
    lines = rows // 128
    slots = idx_v.shape[1]
    chunks = 8
    per = rows // chunks

    def load(i):
        return pltpu.make_async_copy(feat.at[pl.ds(i * per, per)], xb.at[pl.ds(i * per, per)], sem.at[i])

    for i in range(chunks):
        load(i).start()
    count = cnt_s[0]

    kept = jnp.zeros((lines, 128), F32)
    for q in range(slots // 1024):
        ids = idx_v[:, pl.ds(q * 1024, 1024)]
        ids = jnp.where(iota((1, 1024), 1) + q * 1024 < count, ids, -1)
        upper = onehot(iota((lines, 1024), 0) == (ids >> 7))
        lower = onehot(iota((128, 1024), 0) == (ids & 127))
        kept += lax.dot_general(upper, lower, NT, preferred_element_type=F32)

    before = onehot(iota((128, 128), 0) < iota((128, 128), 1))
    above = onehot(iota((lines, lines), 1) < iota((lines, lines), 0))
    upto = onehot(iota((lines, 128), 0) < iota((lines, 128), 1))
    ranks = []
    for k in range(NODES):
        mine = (kept > 0.5) & (node_v[...] == k)
        ones = onehot(mine)
        per_line = jnp.sum(jnp.where(mine, 1.0, 0.0), axis=1, keepdims=True)
        rank = jnp.dot(ones, before, preferred_element_type=F32)
        rank += jnp.dot(above, jnp.broadcast_to(per_line, (lines, 128)).astype(BF16), preferred_element_type=F32)
        ranks.append((mine, rank))
        counts = lax.dot_general(jnp.ones((8, 128), BF16), ones, NT, preferred_element_type=F32)
        starts = jnp.dot(counts.astype(BF16), upto, preferred_element_type=F32)
        offs_v[pl.ds(k, 1), :] = starts[0:1].astype(I32)
    to_scalar = pltpu.make_async_copy(offs_v, offs_s, osem)
    to_scalar.start()

    factor = jnp.where(flag_v[...] == 1, 8.0, 1.0)
    grad = gh[:, 0].reshape(lines, 128) * factor
    hess = gh[:, 1].reshape(lines, 128) * factor
    tpose[...] = jnp.concatenate([grad, hess], axis=0).astype(BF16).astype(F32).T.astype(BF16)

    def clear(t, _):
        z = pl.multiple_of(t * 256, 256)
        xs[pl.ds(z, 256), :] = jnp.zeros((256, width), F32)
        ws[pl.ds(z, 256), :] = jnp.zeros((256, 128), F32)
        return 0

    lax.fori_loop(0, xs.shape[0] // 256, clear, 0)
    acc[...] = jnp.zeros_like(acc)
    exacc[...] = jnp.zeros_like(exacc)
    totacc[...] = jnp.zeros_like(totacc)
    to_scalar.wait()
    sizes = [offs_s[k, lines] for k in range(NODES)]
    bases, blocks = [], []
    base = jnp.int32(0)
    for k in range(NODES):
        bases.append(base)
        blocks.append((sizes[k] + (BLOCK - 1)) // BLOCK)
        base = base + blocks[k] * BLOCK
        mine, rank = ranks[k]
        pos[k] = jnp.where(mine, rank + bases[k].astype(F32), -1.0)

    for i in range(chunks):
        load(i).wait()

    place = iota((WIN, 256), 0).astype(F32).astype(BF16)
    lane = iota((128, 128), 1) & (lines - 1)

    def compact(t, _):
        r0 = pl.multiple_of(t * 256, 256)
        x = xb[pl.ds(r0, 256), :]
        tp = tpose[...]
        zero = jnp.zeros((), BF16)
        wn = jnp.concatenate([jnp.where(lane == 2 * t, tp, zero), jnp.where(lane == 2 * t + 1, tp, zero)], axis=0)
        first, trips = [], jnp.int32(0)
        for k in range(NODES):
            start = bases[k] + offs_s[k, 2 * t]
            stop = bases[k] + offs_s[k, 2 * t + 2]
            a = (start >> 3) << 3
            first.append(a)
            trips = jnp.maximum(trips, jnp.where(stop > start, (stop - a + (WIN - 1)) // WIN, 0))
        prs = [jnp.concatenate([pos[k, pl.ds(2 * t, 1), :], pos[k, pl.ds(2 * t + 1, 1), :]], axis=1) for k in range(NODES)]

        def window(i, _):
            picks = []
            for k in range(NODES):
                d = prs[k] - (first[k] + WIN * i).astype(F32)
                d = jnp.where((d >= 0) & (d < WIN), d, -1.0)
                d = jnp.broadcast_to(d, (WIN, 256)).astype(BF16)
                picks.append(jnp.where(d == place, jnp.ones((), BF16), zero))
            pick = jnp.concatenate(picks, axis=0)
            got = jnp.dot(pick, x, preferred_element_type=F32)
            gotw = jnp.dot(pick, wn, preferred_element_type=F32)
            for k in range(NODES):
                at = pl.ds(pl.multiple_of(first[k] + WIN * i, 8), WIN)
                xs[at, :] += got[k * WIN:(k + 1) * WIN]
                ws[at, :] += gotw[k * WIN:(k + 1) * WIN]
            return 0

        lax.fori_loop(0, trips, window, 0)
        return 0

    lax.fori_loop(0, rows // 256, compact, 0)

    sum_kind = onehot((iota((16, 128), 0) >> 3) == (iota((16, 128), 1) >> 6))
    his = (iota((16, BLOCK), 0) & 7).astype(F32).astype(BF16)
    ramp = (iota((16, BLOCK), 0) + 1).astype(F32).astype(BF16)
    owner = iota((16, 256), 1) >> 4

    def node_loop(k, _):
        base = jnp.where(k == 0, bases[0], jnp.where(k == 1, bases[1], jnp.where(k == 2, bases[2], bases[3])))
        trips = jnp.where(k == 0, blocks[0], jnp.where(k == 1, blocks[1], jnp.where(k == 2, blocks[2], blocks[3])))

        def block(q, _):
            s = pl.multiple_of(base + q * BLOCK, BLOCK)
            x = xs[pl.ds(s, BLOCK), :]
            w16 = lax.dot_general(sum_kind, ws[pl.ds(s, BLOCK), :].astype(BF16), NT, preferred_element_type=F32)
            w16b = w16.astype(BF16)
            w16_s[...] = w16b
            totacc[k] += w16
            exacc[k] += jnp.dot(w16b, onehot(x <= 4.0), preferred_element_type=F32)
            cat = jnp.maximum(jnp.ceil(x.T * 16.0) + 64.0, 0.0)
            hi = jnp.floor(cat * 0.0625)
            hi_s[...] = hi
            lo_s[...] = cat - hi * 16.0 + 1.0

            def group(g, _):
                w16v = w16_s[...]
                f0 = (g >> 1) * 32 + (g & 1)
                a, b = [], []
                for f in range(16):
                    hb = jnp.broadcast_to(hi_s[pl.ds(f0 + 2 * f, 1), :], (16, BLOCK)).astype(BF16)
                    lb = jnp.broadcast_to(lo_s[pl.ds(f0 + 2 * f, 1), :], (16, BLOCK)).astype(BF16)
                    a.append(jnp.where(hb == his, w16v, jnp.zeros((), BF16)))
                    b.append(jnp.minimum(lb, ramp))
                r = lax.dot_general(
                    jnp.concatenate(a, axis=0), jnp.concatenate(b, axis=0), NT, preferred_element_type=F32
                )
                mine = r[0:16]
                for f in range(1, 16):
                    mine = jnp.where(owner == f, r[16 * f:16 * f + 16], mine)
                acc[k, g] += mine
                return 0

            lax.fori_loop(0, width // 16, group, 0, unroll=2)
            return 0

        lax.fori_loop(0, trips, block, 0)
        return 0

    lax.fori_loop(0, NODES, node_loop, 0)

    for j in range(width // 32):
        parts = [acc[k, 2 * j + half, 8 * w:8 * w + 8, :] for half in range(2) for w in range(2) for k in range(NODES)]
        t = jnp.concatenate(parts, axis=0).T
        for z in range(8):
            for c in range(2):
                main[c, z, j] = t[(2 * z + c) * 16:(2 * z + c) * 16 + 16]
    whole = [jnp.sum(totacc[k], axis=1, keepdims=True) for k in range(NODES)]
    lines_ex = [exacc[k, 8 * w:8 * w + 1, :] for w in range(2) for k in range(NODES)]
    lines_ex += [jnp.broadcast_to(whole[k][8 * w:8 * w + 1], (1, width)) for w in range(2) for k in range(NODES)]
    lines_ex.append(jnp.zeros((112, width), F32))
    ext[...] = jnp.concatenate(lines_ex, axis=0).T
    even, odd = ext[pl.ds(0, width // 2, stride=2), :], ext[pl.ds(1, width // 2, stride=2), :]
    both = even + pltpu.roll(odd, 16, 1)
    for j in range(8):
        for z in range(8):
            for c in range(2):
                p = j * 16 + z * 2 + c
                extra[c, z, j] = both[p:p + 1]


def local_histogram(kept_count, features, kept_index, gh, node_ids, sample_flags):
    rows, width = features.shape
    slots = kept_index.shape[0]
    lines = rows // 128
    room = slots + NODES * BLOCK + 512
    return pl.pallas_call(
        hist_body,
        out_shape=(
            jax.ShapeDtypeStruct((2, 8, 8, 16, 128), F32),
            jax.ShapeDtypeStruct((2, 8, 8, 1, 128), F32),
        ),
        in_specs=[SM, HBM, VM, VM, VM, VM],
        out_specs=(VM, VM),
        scratch_shapes=[
            pltpu.VMEM((rows, width), BF16),
            pltpu.VMEM((room, width), F32),
            pltpu.VMEM((room, 128), F32),
            pltpu.VMEM((NODES, lines, 128), F32),
            pltpu.VMEM((128, 128), BF16),
            pltpu.VMEM((width, BLOCK), F32),
            pltpu.VMEM((width, BLOCK), F32),
            pltpu.VMEM((16, BLOCK), BF16),
            pltpu.VMEM((NODES, width // 16, 16, 256), F32),
            pltpu.VMEM((NODES, 16, width), F32),
            pltpu.VMEM((NODES, 16, BLOCK), F32),
            pltpu.VMEM((8, 128), I32),
            pltpu.SMEM((8, 128), I32),
            pltpu.VMEM((width, 128), F32),
            pltpu.SemaphoreType.DMA((8,)),
            pltpu.SemaphoreType.DMA,
        ],
        compiler_params=pltpu.CompilerParams(vmem_limit_bytes=56 << 20),
        name="local_histogram",
    )(
        kept_count,
        features,
        kept_index.reshape(1, slots),
        gh,
        node_ids.reshape(lines, 128),
        sample_flags.reshape(lines, 128),
    )


def gain_body(
    main, extra, edges, gain, rank,
    c1, e1, s1, t1, c2, e2, s2, t2, c3, e3,
    sem1, sem2, sem3,
):
    row, feat = lax.axis_index("rows"), lax.axis_index("feat")
    core, z, y = lax.rem(row, 2), lax.rem(row // 2, 8), row // 16

    def at(yy, zz, cc):
        return (yy * 16 + zz * 2 + cc, feat)

    barrier = pltpu.get_barrier_semaphore()
    pl.semaphore_signal(barrier, inc=1, device_id=at(y, z, 1 - core), device_id_type=MESH)
    for d in range(1, 8):
        pl.semaphore_signal(barrier, inc=1, device_id=at(y, lax.rem(z + d, 8), core), device_id_type=MESH)
        pl.semaphore_signal(barrier, inc=1, device_id=at(lax.rem(y + d, 8), z, core), device_id_type=MESH)
    pl.semaphore_wait(barrier, 15)

    def copy(src, dst, sems, i, w, to):
        return pltpu.make_async_remote_copy(
            src_ref=src, dst_ref=dst, send_sem=sems.at[0, i, w], recv_sem=sems.at[1, i, w],
            device_id=to, device_id_type=MESH,
        )

    other = at(y, z, 1 - core)
    pair = [copy(main.at[1 - core], c1, sem1, 0, 0, other), copy(extra.at[1 - core], e1, sem1, 0, 1, other)]
    for c in pair:
        c.start()
    for c in pair:
        c.wait()

    def add1(i, _):
        s1[i] = main[core, i] + c1[i]
        t1[i] = extra[core, i] + e1[i]
        return 0

    lax.fori_loop(0, 8, add1, 0)

    sends = []
    for d in range(1, 8):
        zz = lax.rem(z + d, 8)
        to = at(y, zz, core)
        sends.append(copy(s1.at[zz], c2.at[d - 1], sem2, d - 1, 0, to))
        sends.append(copy(t1.at[zz], e2.at[d - 1], sem2, d - 1, 1, to))
    for c in sends:
        c.start()
    for c in sends:
        c.wait()

    def add2(i, _):
        a, b = s1[z, i], t1[z, i]
        for d in range(7):
            a += c2[d, i]
            b += e2[d, i]
        s2[i] = a
        t2[i] = b
        return 0

    lax.fori_loop(0, 8, add2, 0)

    sends = []
    for d in range(1, 8):
        yy = lax.rem(y + d, 8)
        to = at(yy, z, core)
        sends.append(copy(s2.at[yy], c3.at[d - 1], sem3, d - 1, 0, to))
        sends.append(copy(t2.at[yy], e3.at[d - 1], sem3, d - 1, 1, to))
    for c in sends:
        c.start()
    for c in sends:
        c.wait()
    a, b = s2[y], t2[y]
    for d in range(7):
        a += c3[d]
        b += e3[d]

    line = iota((16, 128), 0)
    rest = a - jnp.where(line == 0, 0.0, pltpu.roll(a, 1, 0))
    bins = rest - jnp.where(line == 15, 0.0, pltpu.roll(rest, 15, 0))
    hi = iota((16, 128), 1) & 7
    spread = jnp.concatenate([jnp.where(hi == h, bins, 0.0) for h in range(8)], axis=0)
    table = jnp.sum(spread.T.reshape(16, 8, 128), axis=1)
    column = jnp.broadcast_to(b, (128, 128)).T
    for half in range(2):
        e = edges[pl.ds(2 * row + half, 1), :]
        take = jnp.where(iota((128, 128), 0) <= e, 1.0, 0.0)
        left = lax.dot_general(
            table[half * 8:half * 8 + 8], take, (((1,), (0,)), ((), ())),
            precision=lax.Precision.HIGHEST, preferred_element_type=F32,
        )
        left = jnp.where(e >= 128, column[half * 16:half * 16 + 8], left)
        total = column[8:16]
        gl, hl, gs, hs = left[0:4], left[4:8], total[0:4], total[4:8]
        gain[half] = gl * gl / (hl + 1.0) + (gs - gl) * (gs - gl) / (hs - hl + 1.0) - gs * gs / (hs + 1.0)
        rank[half] = hl / hs


def gains(main, extra, cut_edges):
    out = jax.ShapeDtypeStruct((2, NODES, 128), F32)
    return pl.pallas_call(
        gain_body,
        out_shape=(out, out),
        in_specs=[VM, VM, VM],
        out_specs=(VM, VM),
        scratch_shapes=[
            pltpu.VMEM((8, 8, 16, 128), F32),
            pltpu.VMEM((8, 8, 1, 128), F32),
            pltpu.VMEM((8, 8, 16, 128), F32),
            pltpu.VMEM((8, 8, 1, 128), F32),
            pltpu.VMEM((7, 8, 16, 128), F32),
            pltpu.VMEM((7, 8, 1, 128), F32),
            pltpu.VMEM((8, 16, 128), F32),
            pltpu.VMEM((8, 1, 128), F32),
            pltpu.VMEM((7, 16, 128), F32),
            pltpu.VMEM((7, 1, 128), F32),
            pltpu.SemaphoreType.DMA((2, 1, 2)),
            pltpu.SemaphoreType.DMA((2, 7, 2)),
            pltpu.SemaphoreType.DMA((2, 7, 2)),
        ],
        compiler_params=pltpu.CompilerParams(collective_id=1, has_side_effects=True),
        name="gains",
    )(main, extra, cut_edges)


def shards(features, gradients, hessians, node_ids, sample_flags, kept_index, kept_count, cut_edges):
    gh = share(gradients, hessians, lax.axis_size("feat"))
    main, extra = local_histogram(kept_count, features, kept_index, gh, node_ids, sample_flags)
    return gains(main, extra, cut_edges)


def solution(mesh):
    placed = (
        P("rows", "feat"),
        P(("rows", "feat")),
        P(("rows", "feat")),
        P("rows"),
        P("rows"),
        P("rows"),
        P("rows"),
        P("feat", None),
    )
    return jax.shard_map(
        shards,
        mesh=mesh,
        in_specs=placed,
        out_specs=(P(("feat", "rows"), None, None), P(("feat", "rows"), None, None)),
        check_vma=False,
    )
```

time: 619 us -> 106 us (0.17)
  blocking collectives: 279 us -> 0 us
  local copies, waits for them, and re-layouts: 146 us -> 2.54 us
  Pallas kernels: 0 us -> 102 us
  other arithmetic: 89.7 us -> 0 us
  matrix products: 76 us -> 0 us
  between operations: 14.8 us -> 1.3 us
  loops' own time: 12.7 us -> 0 us
    psum x1 -> x0, blocking collectives: 260 us -> none  [shards(): lax.psum((histogram(kept_columns, kept_weights, cut_values), jnp.sum(kept...]
    gather x5 -> x0, local copies, waits for them, and re-layouts: 108 us -> none  [the longest x1 23 us: shards(): sample_flags[kept_index] == 1]
    pallas_call x0 -> x3, Pallas kernels: none -> 102 us  [the longest x1 71.5 us: gains(): pl.pallas_call(gain_body, out_shape=(out, out), in_specs=[VM, VM, VM], ou...]
    le x64 -> x0, other arithmetic: 86.2 us -> none  [add_slots(): slot_part.astype(jnp.float32)[:, None, :] <= block_cuts[:, :, None]]
    dot_general x64 -> x0, matrix products: 76 us -> none  [add_slots(): lax.dot_general(weight_part, compare, (((1,), (1,)), ((), ())), preferred...]
    dynamic_slice x48 -> x0, local copies, waits for them, and re-layouts: 25.3 us -> none  [the longest x16 14.7 us: feature_block(): lax.dynamic_slice_in_dim(kept_columns, i * feature_width, feature_width, 0)]
    all_gather x2 -> x0, blocking collectives: 19.2 us -> none  [the longest x1 10.2 us: shards(): lax.all_gather(gradients, 'feat', axis=0, tiled=True)]
    another operation x17 -> x0, loops' own time: 12.7 us -> none  [the longest x1 11.3 us: histogram(): lax.map(feature_block, jnp.arange(feature_count // feature_width, dtype=j...]
  transfers between devices with their start and end apart: 1 -> 0, of which waited for: 0 -> 0; matrix products, arithmetic and copies ran while one was open for 0% -> 0% of each run, Pallas kernels for 0% -> 0%
where the time goes in v1:
time: 106 us
  Pallas kernels  102 us (96%)
  local copies, waits for them, and re-layouts  2.54 us (2%)
  between operations  1.3 us (1%)
    pallas_call x1, Pallas kernels, gains(): pl.pallas_call(gain_body, out_shape=(out, out), in_specs=[VM, VM, VM], ou...  71.5 us
    pallas_call x1, Pallas kernels, local_histogram(): pl.pallas_call(hist_body, out_shape=(jax.ShapeDtypeStruct((2, 8, 8, 16, 1...  22.7 us
    pallas_call x1, Pallas kernels, share(): pl.pallas_call(functools.partial(share_body, peers), out_shape=jax.ShapeD...  7.95 us
    unnamed x2, local copies, waits for them, and re-layouts  2.54 us

profile of v1, /device:TPU:1, one launch (start us, length us, event | category | flops | bytes accessed | tf_op | source)
XLA Modules:
  0.0 106.0 jit_solution(14896726246538388459)
XLA Ops:
  1.3 8.0 %share.1.gh = f32[4,2,16,128]{3,2,1,0:T(8,128)} custom-call(f32[16,128]{1,0:T(8,128)} %bitcast.8, f32[16,128]{1,0:T(8,128)} %bitcast.9), custom_call_target="tpu_custom_call" | custom-call | tf_op jit(solution)/shard_map/share/pallas_call | solution.py:59
  9.2 22.7 %local_histogram.1 = (f32[2,8,8,16,128]{4,3,2,1,0:T(8,128)}, f32[2,8,8,1,128]{4,3,2,1,0:T(1,128)}) custom-call(s32[1]{0:T(128)S(6)} %copy.12.cnt_s, bf16[8192,256]{1,0:T(8,128)(2,1)} %feat.1, s32[1,4096]{1,0:T(1,128)} %bitcast.7, f32[4,2,16,128]{3,2,1,0:T(8,128)} %share.1.gh, s32[64,128]{1,0:T(8,128)} %bitcast.5, s32[64,128]{1,0:T(8,128)} %bitcast.6), custom_call_target="tpu_custom_call" | custom-call | tf_op jit(solution)/shard_map/local_histogram/pallas_call | solution.py:253
  31.9 71.5 %gains.1 = (f32[2,4,128]{2,1,0:T(4,128)}, f32[2,4,128]{2,1,0:T(4,128)}) custom-call(f32[2,8,8,16,128]{4,3,2,1,0:T(8,128)} %get-tuple-element.4.main, f32[2,8,8,1,128]{4,3,2,1,0:T(1,128)} %get-tuple-element.5.extra, s32[256,128]{1,0:T(8,128)} %edges.1), custom_call_target="tpu_custom_call" | custom-call | tf_op jit(solution)/shard_map/gains/pallas_call | solution.py:389
  103.4 1.3 %copy.13 = f32[2,4,128]{2,1,0:T(4,128)} copy(f32[2,4,128]{2,1,0:T(4,128)} %get-tuple-element.8) | data formatting | bytes 8192
  104.7 1.3 %copy.14 = f32[2,4,128]{2,1,0:T(4,128)} copy(f32[2,4,128]{2,1,0:T(4,128)} %get-tuple-element.9) | data formatting | bytes 8192

commit v2 on v1

--- a/solution.py
+++ b/solution.py
@@ -68,7 +68,7 @@
 
 
 def hist_body(
-    cnt_s, feat, idx_v, gh, node_v, flag_v, main, extra,
+    cnt_s, feat, idx_v, gh, node_v, flag_v, main_z, main_y, extra,
     xb, xs, ws, pos, tpose, hi_s, lo_s, w16_s, acc, exacc, totacc, offs_v, offs_s, ext, sem, osem,
 ):
     rows, width = feat.shape
@@ -141,41 +141,58 @@
     place = iota((WIN, 256), 0).astype(F32).astype(BF16)
     lane = iota((128, 128), 1) & (lines - 1)
 
-    def compact(t, _):
+    zero = jnp.zeros((), BF16)
+
+    def line_of(t):
         r0 = pl.multiple_of(t * 256, 256)
         x = xb[pl.ds(r0, 256), :]
         tp = tpose[...]
-        zero = jnp.zeros((), BF16)
         wn = jnp.concatenate([jnp.where(lane == 2 * t, tp, zero), jnp.where(lane == 2 * t + 1, tp, zero)], axis=0)
-        first, trips = [], jnp.int32(0)
+        first, trips = [], jnp.int32(1)
         for k in range(NODES):
             start = bases[k] + offs_s[k, 2 * t]
             stop = bases[k] + offs_s[k, 2 * t + 2]
             a = (start >> 3) << 3
             first.append(a)
-            trips = jnp.maximum(trips, jnp.where(stop > start, (stop - a + (WIN - 1)) // WIN, 0))
-        prs = [jnp.concatenate([pos[k, pl.ds(2 * t, 1), :], pos[k, pl.ds(2 * t + 1, 1), :]], axis=1) for k in range(NODES)]
-
-        def window(i, _):
-            picks = []
-            for k in range(NODES):
-                d = prs[k] - (first[k] + WIN * i).astype(F32)
-                d = jnp.where((d >= 0) & (d < WIN), d, -1.0)
-                d = jnp.broadcast_to(d, (WIN, 256)).astype(BF16)
-                picks.append(jnp.where(d == place, jnp.ones((), BF16), zero))
-            pick = jnp.concatenate(picks, axis=0)
-            got = jnp.dot(pick, x, preferred_element_type=F32)
-            gotw = jnp.dot(pick, wn, preferred_element_type=F32)
-            for k in range(NODES):
-                at = pl.ds(pl.multiple_of(first[k] + WIN * i, 8), WIN)
-                xs[at, :] += got[k * WIN:(k + 1) * WIN]
-                ws[at, :] += gotw[k * WIN:(k + 1) * WIN]
+            trips = jnp.maximum(trips, (stop - a + (WIN - 1)) >> 6)
+        return x, wn, first, trips
+
+    def window(t, i, x, wn, first):
+        picks = []
+        for k in range(NODES):
+            pr = jnp.concatenate([pos[k, pl.ds(2 * t, 1), :], pos[k, pl.ds(2 * t + 1, 1), :]], axis=1)
+            d = pr - (first[k] + WIN * i).astype(F32)
+            d = jnp.where((d >= 0) & (d < WIN), d, -1.0)
+            d = jnp.broadcast_to(d, (WIN, 256)).astype(BF16)
+            picks.append(jnp.where(d == place, jnp.ones((), BF16), zero))
+        pick = jnp.concatenate(picks, axis=0)
+        got = jnp.dot(pick, x, preferred_element_type=F32)
+        gotw = jnp.dot(pick, wn, preferred_element_type=F32)
+        for k in range(NODES):
+            at = pl.ds(pl.multiple_of(first[k] + WIN * i, 8), WIN)
+            xs[at, :] += got[k * WIN:(k + 1) * WIN]
+            ws[at, :] += gotw[k * WIN:(k + 1) * WIN]
+
+    def compact(t, most):
+        x, wn, first, trips = line_of(t)
+        window(t, 0, x, wn, first)
+        return jnp.maximum(most, trips)
+
+    most = lax.fori_loop(0, rows // 256, compact, jnp.int32(1), unroll=4)
+
+    @pl.when(most > 1)
+    def _():
+        def more(t, _):
+            x, wn, first, trips = line_of(t)
+
+            def further(i, _):
+                window(t, i, x, wn, first)
+                return 0
+
+            lax.fori_loop(1, trips, further, 0)
             return 0
 
-        lax.fori_loop(0, trips, window, 0)
-        return 0
-
-    lax.fori_loop(0, rows // 256, compact, 0)
+        lax.fori_loop(0, rows // 256, more, 0)
 
     sum_kind = onehot((iota((16, 128), 0) >> 3) == (iota((16, 128), 1) >> 6))
     his = (iota((16, BLOCK), 0) & 7).astype(F32).astype(BF16)
@@ -217,7 +234,7 @@
                 acc[k, g] += mine
                 return 0
 
-            lax.fori_loop(0, width // 16, group, 0, unroll=2)
+            lax.fori_loop(0, width // 16, group, 0, unroll=16)
             return 0
 
         lax.fori_loop(0, trips, block, 0)
@@ -230,7 +247,8 @@
         t = jnp.concatenate(parts, axis=0).T
         for z in range(8):
             for c in range(2):
-                main[c, z, j] = t[(2 * z + c) * 16:(2 * z + c) * 16 + 16]
+                main_z[c, z, j] = t[(2 * z + c) * 16:(2 * z + c) * 16 + 8]
+                main_y[c, j, z] = t[(2 * z + c) * 16 + 8:(2 * z + c) * 16 + 16]
     whole = [jnp.sum(totacc[k], axis=1, keepdims=True) for k in range(NODES)]
     lines_ex = [exacc[k, 8 * w:8 * w + 1, :] for w in range(2) for k in range(NODES)]
     lines_ex += [jnp.broadcast_to(whole[k][8 * w:8 * w + 1], (1, width)) for w in range(2) for k in range(NODES)]
@@ -253,11 +271,12 @@
     return pl.pallas_call(
         hist_body,
         out_shape=(
-            jax.ShapeDtypeStruct((2, 8, 8, 16, 128), F32),
+            jax.ShapeDtypeStruct((2, 8, 8, 8, 128), F32),
+            jax.ShapeDtypeStruct((2, 8, 8, 8, 128), F32),
             jax.ShapeDtypeStruct((2, 8, 8, 1, 128), F32),
         ),
         in_specs=[SM, HBM, VM, VM, VM, VM],
-        out_specs=(VM, VM),
+        out_specs=(VM, VM, VM),
         scratch_shapes=[
             pltpu.VMEM((rows, width), BF16),
             pltpu.VMEM((room, width), F32),
@@ -288,9 +307,12 @@
     )
 
 
-def gain_body(
-    main, extra, edges, gain, rank,
-    c1, e1, s1, t1, c2, e2, s2, t2, c3, e3,
+FAR_FIRST = (4, 3, 5, 2, 6, 1, 7)
+
+
+def reduce_body(
+    main_z, main_y, extra, edges, out,
+    cz, cy, ce, sz, sy, se, rz, ry, re, uz, uy, ue, vz, vy, ve,
     sem1, sem2, sem3,
 ):
     row, feat = lax.axis_index("rows"), lax.axis_index("feat")
@@ -299,11 +321,14 @@
     def at(yy, zz, cc):
         return (yy * 16 + zz * 2 + cc, feat)
 
+    other = at(y, z, 1 - core)
+    to_z = {d: at(y, lax.rem(z + d, 8), core) for d in FAR_FIRST}
+    to_y = {d: at(lax.rem(y + d, 8), z, core) for d in FAR_FIRST}
     barrier = pltpu.get_barrier_semaphore()
-    pl.semaphore_signal(barrier, inc=1, device_id=at(y, z, 1 - core), device_id_type=MESH)
-    for d in range(1, 8):
-        pl.semaphore_signal(barrier, inc=1, device_id=at(y, lax.rem(z + d, 8), core), device_id_type=MESH)
-        pl.semaphore_signal(barrier, inc=1, device_id=at(lax.rem(y + d, 8), z, core), device_id_type=MESH)
+    pl.semaphore_signal(barrier, inc=1, device_id=other, device_id_type=MESH)
+    for d in FAR_FIRST:
+        pl.semaphore_signal(barrier, inc=1, device_id=to_z[d], device_id_type=MESH)
+        pl.semaphore_signal(barrier, inc=1, device_id=to_y[d], device_id_type=MESH)
     pl.semaphore_wait(barrier, 15)
 
     def copy(src, dst, sems, i, w, to):
@@ -312,57 +337,89 @@
             device_id=to, device_id_type=MESH,
         )
 
-    other = at(y, z, 1 - core)
-    pair = [copy(main.at[1 - core], c1, sem1, 0, 0, other), copy(extra.at[1 - core], e1, sem1, 0, 1, other)]
-    for c in pair:
-        c.start()
-    for c in pair:
-        c.wait()
-
-    def add1(i, _):
-        s1[i] = main[core, i] + c1[i]
-        t1[i] = extra[core, i] + e1[i]
-        return 0
-
-    lax.fori_loop(0, 8, add1, 0)
-
-    sends = []
-    for d in range(1, 8):
-        zz = lax.rem(z + d, 8)
-        to = at(y, zz, core)
-        sends.append(copy(s1.at[zz], c2.at[d - 1], sem2, d - 1, 0, to))
-        sends.append(copy(t1.at[zz], e2.at[d - 1], sem2, d - 1, 1, to))
-    for c in sends:
-        c.start()
-    for c in sends:
-        c.wait()
-
-    def add2(i, _):
-        a, b = s1[z, i], t1[z, i]
-        for d in range(7):
-            a += c2[d, i]
-            b += e2[d, i]
-        s2[i] = a
-        t2[i] = b
-        return 0
-
-    lax.fori_loop(0, 8, add2, 0)
-
-    sends = []
-    for d in range(1, 8):
-        yy = lax.rem(y + d, 8)
-        to = at(yy, z, core)
-        sends.append(copy(s2.at[yy], c3.at[d - 1], sem3, d - 1, 0, to))
-        sends.append(copy(t2.at[yy], e3.at[d - 1], sem3, d - 1, 1, to))
-    for c in sends:
-        c.start()
-    for c in sends:
-        c.wait()
-    a, b = s2[y], t2[y]
-    for d in range(7):
-        a += c3[d]
-        b += e3[d]
-
+    pair = {}
+    for d in FAR_FIRST + (0,):
+        zz, yy = lax.rem(z + d, 8), lax.rem(y + d, 8)
+        pair[d] = (
+            copy(main_z.at[1 - core, zz], cz.at[zz], sem1, d, 0, other),
+            copy(main_y.at[1 - core, yy], cy.at[yy], sem1, d, 1, other),
+            copy(extra.at[1 - core, zz], ce.at[zz], sem1, d, 2, other),
+        )
+        for c in pair[d]:
+            c.start()
+
+    first = {}
+    for d in FAR_FIRST + (0,):
+        zz, yy = lax.rem(z + d, 8), lax.rem(y + d, 8)
+        for c in pair[d]:
+            c.wait_recv()
+        sz[zz] = main_z[core, zz] + cz[zz]
+        sy[yy] = main_y[core, yy] + cy[yy]
+        se[zz] = extra[core, zz] + ce[zz]
+        if d:
+            first[d] = (
+                copy(sz.at[zz], rz.at[d - 1], sem2, d - 1, 0, to_z[d]),
+                copy(sy.at[yy], ry.at[d - 1], sem2, d - 1, 1, to_y[d]),
+                copy(se.at[zz], re.at[d - 1], sem2, d - 1, 2, to_z[d]),
+            )
+            for c in first[d]:
+                c.start()
+    az, ay, ae = sz[z], sy[y], se[z]
+    for d in FAR_FIRST[::-1]:
+        for c in first[d]:
+            c.wait_recv()
+        az += rz[d - 1]
+        ay += ry[d - 1]
+        ae += re[d - 1]
+    uz[...] = az
+    uy[...] = ay
+    ue[...] = ae
+
+    second = {}
+    for d in FAR_FIRST:
+        zz, yy = lax.rem(z + d, 8), lax.rem(y + d, 8)
+        second[d] = (
+            copy(uz.at[yy], vz.at[d - 1], sem3, d - 1, 0, to_y[d]),
+            copy(uy.at[zz], vy.at[d - 1], sem3, d - 1, 1, to_z[d]),
+            copy(ue.at[yy], ve.at[d - 1], sem3, d - 1, 2, to_y[d]),
+        )
+        for c in second[d]:
+            c.start()
+    a, b, e = uz[y], uy[z], ue[y]
+    for d in FAR_FIRST[::-1]:
+        for c in second[d]:
+            c.wait_recv()
+        a += vz[d - 1]
+        b += vy[d - 1]
+        e += ve[d - 1]
+    out[pl.ds(0, 8), :] = a
+    out[pl.ds(8, 8), :] = b
+    out[pl.ds(16, 1), :] = e
+    out[pl.ds(17, 2), :] = edges[pl.ds(2 * row, 2), :].astype(F32)
+    for c in [c for group in (pair, first, second) for some in group.values() for c in some]:
+        c.wait_send()
+
+
+def reduce_rows(main_z, main_y, extra, cut_edges):
+    big, small = (8, 8, 8, 128), (8, 8, 1, 128)
+    return pl.pallas_call(
+        reduce_body,
+        out_shape=jax.ShapeDtypeStruct((24, 128), F32),
+        in_specs=[VM] * 4,
+        out_specs=VM,
+        scratch_shapes=[pltpu.VMEM(s, F32) for s in (big, big, small, big, big, small)]
+        + [pltpu.VMEM((7,) + s[1:], F32) for s in (big, big, small)]
+        + [pltpu.VMEM(s[1:], F32) for s in (big, big, small)]
+        + [pltpu.VMEM((7,) + s[2:], F32) for s in (big, big, small)]
+        + [pltpu.SemaphoreType.DMA((2, n, 3)) for n in (8, 7, 7)],
+        compiler_params=pltpu.CompilerParams(collective_id=1, has_side_effects=True),
+        name="reduce_rows",
+    )(main_z, main_y, extra, cut_edges)
+
+
+def gain_body(sums, gain, rank):
+    a = sums[pl.ds(0, 16), :]
+    b = sums[pl.ds(16, 1), :]
     line = iota((16, 128), 0)
     rest = a - jnp.where(line == 0, 0.0, pltpu.roll(a, 1, 0))
     bins = rest - jnp.where(line == 15, 0.0, pltpu.roll(rest, 15, 0))
@@ -371,50 +428,28 @@
     table = jnp.sum(spread.T.reshape(16, 8, 128), axis=1)
     column = jnp.broadcast_to(b, (128, 128)).T
     for half in range(2):
-        e = edges[pl.ds(2 * row + half, 1), :]
-        take = jnp.where(iota((128, 128), 0) <= e, 1.0, 0.0)
+        e = sums[pl.ds(17 + half, 1), :]
+        take = jnp.where(iota((128, 128), 0).astype(F32) <= e, 1.0, 0.0)
         left = lax.dot_general(
             table[half * 8:half * 8 + 8], take, (((1,), (0,)), ((), ())),
             precision=lax.Precision.HIGHEST, preferred_element_type=F32,
         )
-        left = jnp.where(e >= 128, column[half * 16:half * 16 + 8], left)
+        left = jnp.where(e >= 128.0, column[half * 16:half * 16 + 8], left)
         total = column[8:16]
         gl, hl, gs, hs = left[0:4], left[4:8], total[0:4], total[4:8]
         gain[half] = gl * gl / (hl + 1.0) + (gs - gl) * (gs - gl) / (hs - hl + 1.0) - gs * gs / (hs + 1.0)
         rank[half] = hl / hs
 
 
-def gains(main, extra, cut_edges):
+def gains(sums):
     out = jax.ShapeDtypeStruct((2, NODES, 128), F32)
-    return pl.pallas_call(
-        gain_body,
-        out_shape=(out, out),
-        in_specs=[VM, VM, VM],
-        out_specs=(VM, VM),
-        scratch_shapes=[
-            pltpu.VMEM((8, 8, 16, 128), F32),
-            pltpu.VMEM((8, 8, 1, 128), F32),
-            pltpu.VMEM((8, 8, 16, 128), F32),
-            pltpu.VMEM((8, 8, 1, 128), F32),
-            pltpu.VMEM((7, 8, 16, 128), F32),
-            pltpu.VMEM((7, 8, 1, 128), F32),
-            pltpu.VMEM((8, 16, 128), F32),
-            pltpu.VMEM((8, 1, 128), F32),
-            pltpu.VMEM((7, 16, 128), F32),
-            pltpu.VMEM((7, 1, 128), F32),
-            pltpu.SemaphoreType.DMA((2, 1, 2)),
-            pltpu.SemaphoreType.DMA((2, 7, 2)),
-            pltpu.SemaphoreType.DMA((2, 7, 2)),
-        ],
-        compiler_params=pltpu.CompilerParams(collective_id=1, has_side_effects=True),
-        name="gains",
-    )(main, extra, cut_edges)
+    return pl.pallas_call(gain_body, out_shape=(out, out), in_specs=[VM], out_specs=(VM, VM), name="gains")(sums)
 
 
 def shards(features, gradients, hessians, node_ids, sample_flags, kept_index, kept_count, cut_edges):
     gh = share(gradients, hessians, lax.axis_size("feat"))
-    main, extra = local_histogram(kept_count, features, kept_index, gh, node_ids, sample_flags)
-    return gains(main, extra, cut_edges)
+    main_z, main_y, extra = local_histogram(kept_count, features, kept_index, gh, node_ids, sample_flags)
+    return gains(reduce_rows(main_z, main_y, extra, cut_edges))
 
 
 def solution(mesh):

time: 106 us -> 64.5 us (0.61)
  Pallas kernels: 102 us -> 62.6 us
  local copies, waits for them, and re-layouts: 2.54 us -> 0 us
    pallas_call x2 -> x3, Pallas kernels: 94.2 us -> 54.6 us  [the longest x1 41.5 us: reduce_rows(): pl.pallas_call(reduce_body, out_shape=jax.ShapeDtypeStruct((24, 128), F32...]
    unnamed x2 -> x0, local copies, waits for them, and re-layouts: 2.54 us -> none
where the time goes in v2:
time: 64.5 us; the launch traced here: 63.9 us
  Pallas kernels  62.6 us (97%)
  between operations  1.3 us (2%)
    pallas_call x1, Pallas kernels, reduce_rows(): pl.pallas_call(reduce_body, out_shape=jax.ShapeDtypeStruct((24, 128), F32...  41.5 us
    pallas_call x1, Pallas kernels, local_histogram(): pl.pallas_call(hist_body, out_shape=(jax.ShapeDtypeStruct((2, 8, 8, 8, 12...  11.5 us
    pallas_call x1, Pallas kernels, share(): pl.pallas_call(functools.partial(share_body, peers), out_shape=jax.ShapeD...  7.95 us
    pallas_call x1, Pallas kernels, gains(): pl.pallas_call(gain_body, out_shape=(out, out), in_specs=[VM], out_specs=...  1.63 us

profile of v2, /device:TPU:1, one launch (start us, length us, event | category | flops | bytes accessed | tf_op | source)
XLA Modules:
  0.0 63.9 jit_solution(2127026270580737275)
XLA Ops:
  1.3 8.0 %share.1.gh = f32[4,2,16,128]{3,2,1,0:T(8,128)} custom-call(f32[16,128]{1,0:T(8,128)} %bitcast.8, f32[16,128]{1,0:T(8,128)} %bitcast.9), custom_call_target="tpu_custom_call" | custom-call | tf_op jit(solution)/shard_map/share/pallas_call | solution.py:59
  9.2 11.5 %local_histogram.1 = (f32[2,8,8,8,128]{4,3,2,1,0:T(8,128)}, f32[2,8,8,8,128]{4,3,2,1,0:T(8,128)}, f32[2,8,8,1,128]{4,3,2,1,0:T(1,128)}) custom-call(s32[1]{0:T(128)S(6)} %copy.10.cnt_s, bf16[8192,256]{1,0:T(8,128)(2,1)} %feat.1, s32[1,4096]{1,0:T(1,128)} %bitcast.7, f32[4,2,16,128]{3,2,1,0:T(8,128)} %share.1.gh, s32[64,128]{1,0:T(8,128)} %bitcast.5, ...), custom_call_target="tpu_custom_call" | custom-call | tf_op jit(solution)/shard_map/local_histogram/pallas_call | solution.py:271
  20.8 41.5 %reduce_rows.1.sums = f32[24,128]{1,0:T(8,128)} custom-call(f32[2,8,8,8,128]{4,3,2,1,0:T(8,128)} %get-tuple-element.5.main_z, f32[2,8,8,8,128]{4,3,2,1,0:T(8,128)} %get-tuple-element.6.main_y, f32[2,8,8,1,128]{4,3,2,1,0:T(1,128)} %get-tuple-element.7.extra, s32[256,128]{1,0:T(8,128)} %edges.1), custom_call_target="tpu_custom_call" | custom-call | tf_op jit(solution)/shard_map/reduce_rows/pallas_call | solution.py:405
  62.3 1.6 %gains.1 = (f32[2,4,128]{2,1,0:T(4,128)}, f32[2,4,128]{2,1,0:T(4,128)}) custom-call(f32[24,128]{1,0:T(8,128)} %reduce_rows.1.sums), custom_call_target="tpu_custom_call" | custom-call | tf_op jit(solution)/shard_map/gains/pallas_call | solution.py:446

commit v3 on v2

--- a/solution.py
+++ b/solution.py
@@ -26,15 +26,13 @@
     return jnp.where(cond, 1.0, 0.0).astype(BF16)
 
 
-def share_body(peers, g_ref, h_ref, out_ref, send_sem, recv_sem):
+def share_body(peers, g_ref, h_ref, out_ref, send_sem, recv_sem, own_sem):
     row, me = lax.axis_index("rows"), lax.axis_index("feat")
     barrier = pltpu.get_barrier_semaphore()
     for d in range(1, peers):
         pl.semaphore_signal(barrier, inc=1, device_id=(row, lax.rem(me + d, peers)), device_id_type=MESH)
-    out_ref[me, 0] = g_ref[...]
-    out_ref[me, 1] = h_ref[...]
+    copies = [pltpu.make_async_copy(ref, out_ref.at[me, w], own_sem.at[w]) for w, ref in enumerate((g_ref, h_ref))]
     pl.semaphore_wait(barrier, peers - 1)
-    copies = []
     for d in range(1, peers):
         to = (row, lax.rem(me + d, peers))
         for w, ref in enumerate((g_ref, h_ref)):
@@ -59,29 +57,22 @@
     return pl.pallas_call(
         functools.partial(share_body, peers),
         out_shape=jax.ShapeDtypeStruct((peers, 2, part // 128, 128), F32),
-        in_specs=[VM, VM],
+        in_specs=[pl.BlockSpec(memory_space=pltpu.HBM)] * 2,
         out_specs=VM,
-        scratch_shapes=[pltpu.SemaphoreType.DMA((peers, 2)), pltpu.SemaphoreType.DMA((peers, 2))],
-        compiler_params=pltpu.CompilerParams(collective_id=0, has_side_effects=True),
+        scratch_shapes=[pltpu.SemaphoreType.DMA(n) for n in ((peers, 2), (peers, 2), (2,))],
+        compiler_params=pltpu.CompilerParams(collective_id=0, has_side_effects=True, vmem_limit_bytes=4 << 20),
+        cost_estimate=pl.CostEstimate(flops=5_000_000_000, bytes_accessed=8_000_000, transcendentals=0),
         name="share",
     )(gradients.reshape(part // 128, 128), hessians.reshape(part // 128, 128))
 
 
 def hist_body(
     cnt_s, feat, idx_v, gh, node_v, flag_v, main_z, main_y, extra,
-    xb, xs, ws, pos, tpose, hi_s, lo_s, w16_s, acc, exacc, totacc, offs_v, offs_s, ext, sem, osem,
+    xs, ws, pos, tpose, hi_a, lo_a, w16_a, hi_b, lo_b, w16_b, acc, exacc, totacc, offs_v, offs_s, ext, osem,
 ):
     rows, width = feat.shape
     lines = rows // 128
     slots = idx_v.shape[1]
-    chunks = 8
-    per = rows // chunks
-
-    def load(i):
-        return pltpu.make_async_copy(feat.at[pl.ds(i * per, per)], xb.at[pl.ds(i * per, per)], sem.at[i])
-
-    for i in range(chunks):
-        load(i).start()
     count = cnt_s[0]
 
     kept = jnp.zeros((lines, 128), F32)
@@ -135,9 +126,6 @@
         mine, rank = ranks[k]
         pos[k] = jnp.where(mine, rank + bases[k].astype(F32), -1.0)
 
-    for i in range(chunks):
-        load(i).wait()
-
     place = iota((WIN, 256), 0).astype(F32).astype(BF16)
     lane = iota((128, 128), 1) & (lines - 1)
 
@@ -145,7 +133,7 @@
 
     def line_of(t):
         r0 = pl.multiple_of(t * 256, 256)
-        x = xb[pl.ds(r0, 256), :]
+        x = feat[pl.ds(r0, 256), :]
         tp = tpose[...]
         wn = jnp.concatenate([jnp.where(lane == 2 * t, tp, zero), jnp.where(lane == 2 * t + 1, tp, zero)], axis=0)
         first, trips = [], jnp.int32(1)
@@ -173,12 +161,16 @@
             xs[at, :] += got[k * WIN:(k + 1) * WIN]
             ws[at, :] += gotw[k * WIN:(k + 1) * WIN]
 
-    def compact(t, most):
-        x, wn, first, trips = line_of(t)
-        window(t, 0, x, wn, first)
-        return jnp.maximum(most, trips)
-
-    most = lax.fori_loop(0, rows // 256, compact, jnp.int32(1), unroll=4)
+    each = 8
+
+    def compact(i, most):
+        for u in range(each):
+            x, wn, first, trips = line_of(i * each + u)
+            window(i * each + u, 0, x, wn, first)
+            most = jnp.maximum(most, trips)
+        return most
+
+    most = lax.fori_loop(0, rows // 256 // each, compact, jnp.int32(1))
 
     @pl.when(most > 1)
     def _():
@@ -194,57 +186,68 @@
 
         lax.fori_loop(0, rows // 256, more, 0)
 
-    sum_kind = onehot((iota((16, 128), 0) >> 3) == (iota((16, 128), 1) >> 6))
     his = (iota((16, BLOCK), 0) & 7).astype(F32).astype(BF16)
     ramp = (iota((16, BLOCK), 0) + 1).astype(F32).astype(BF16)
     owner = iota((16, 256), 1) >> 4
-
-    def node_loop(k, _):
-        base = jnp.where(k == 0, bases[0], jnp.where(k == 1, bases[1], jnp.where(k == 2, bases[2], bases[3])))
-        trips = jnp.where(k == 0, blocks[0], jnp.where(k == 1, blocks[1], jnp.where(k == 2, blocks[2], blocks[3])))
-
-        def block(q, _):
-            s = pl.multiple_of(base + q * BLOCK, BLOCK)
-            x = xs[pl.ds(s, BLOCK), :]
-            w16 = lax.dot_general(sum_kind, ws[pl.ds(s, BLOCK), :].astype(BF16), NT, preferred_element_type=F32)
-            w16b = w16.astype(BF16)
-            w16_s[...] = w16b
-            totacc[k] += w16
-            exacc[k] += jnp.dot(w16b, onehot(x <= 4.0), preferred_element_type=F32)
-            cat = jnp.maximum(jnp.ceil(x.T * 16.0) + 64.0, 0.0)
-            hi = jnp.floor(cat * 0.0625)
-            hi_s[...] = hi
-            lo_s[...] = cat - hi * 16.0 + 1.0
-
-            def group(g, _):
-                w16v = w16_s[...]
-                f0 = (g >> 1) * 32 + (g & 1)
-                a, b = [], []
-                for f in range(16):
-                    hb = jnp.broadcast_to(hi_s[pl.ds(f0 + 2 * f, 1), :], (16, BLOCK)).astype(BF16)
-                    lb = jnp.broadcast_to(lo_s[pl.ds(f0 + 2 * f, 1), :], (16, BLOCK)).astype(BF16)
-                    a.append(jnp.where(hb == his, w16v, jnp.zeros((), BF16)))
-                    b.append(jnp.minimum(lb, ramp))
-                r = lax.dot_general(
-                    jnp.concatenate(a, axis=0), jnp.concatenate(b, axis=0), NT, preferred_element_type=F32
-                )
-                mine = r[0:16]
-                for f in range(1, 16):
-                    mine = jnp.where(owner == f, r[16 * f:16 * f + 16], mine)
-                acc[k, g] += mine
-                return 0
-
-            lax.fori_loop(0, width // 16, group, 0, unroll=16)
-            return 0
-
-        lax.fori_loop(0, trips, block, 0)
+    ends = [blocks[0], blocks[0] + blocks[1], blocks[0] + blocks[1] + blocks[2]]
+    all_blocks = ends[2] + blocks[3]
+
+    def node_at(q):
+        return sum((q >= end).astype(I32) for end in ends)
+
+    def prepare(q, hi_s, lo_s, w16_s):
+        k = node_at(q)
+        s = pl.multiple_of(q * BLOCK, BLOCK)
+        x = xs[pl.ds(s, BLOCK), :]
+        wt = ws[pl.ds(s, BLOCK), :].T
+        w16 = jnp.concatenate(
+            [jnp.broadcast_to(jnp.sum(wt[64 * w:64 * w + 64], axis=0, keepdims=True), (8, BLOCK)) for w in range(2)], axis=0
+        )
+        w16b = w16.astype(BF16)
+        w16_s[...] = w16b
+        totacc[k] += w16
+        exacc[k] += jnp.dot(w16b, onehot(x <= 4.0), preferred_element_type=F32)
+        cat = jnp.maximum(jnp.ceil(x.T * 16.0) + 64.0, 0.0)
+        hi = jnp.floor(cat * 0.0625)
+        hi_s[...] = hi
+        lo_s[...] = cat - hi * 16.0 + 1.0
+
+    def groups(q, hi_s, lo_s, w16_s):
+        k = node_at(q)
+        w16v = w16_s[...]
+        for g in range(width // 16):
+            f0 = (g >> 1) * 32 + (g & 1)
+            a, b = [], []
+            for f in range(16):
+                hb = jnp.broadcast_to(hi_s[f0 + 2 * f:f0 + 2 * f + 1, :], (16, BLOCK)).astype(BF16)
+                lb = jnp.broadcast_to(lo_s[f0 + 2 * f:f0 + 2 * f + 1, :], (16, BLOCK)).astype(BF16)
+                a.append(jnp.where(hb == his, w16v, jnp.zeros((), BF16)))
+                b.append(jnp.minimum(lb, ramp))
+            r = lax.dot_general(jnp.concatenate(a, axis=0), jnp.concatenate(b, axis=0), NT, preferred_element_type=F32)
+            mine = r[0:16]
+            for f in range(1, 16):
+                mine = jnp.where(owner == f, r[16 * f:16 * f + 16], mine)
+            acc[k, g] += mine
+
+    one, two = (hi_a, lo_a, w16_a), (hi_b, lo_b, w16_b)
+    prepare(jnp.int32(0), *one)
+
+    def blocks_of_two(i, _):
+        q = 2 * i
+        prepare(q + 1, *two)
+        groups(q, *one)
+        prepare(q + 2, *one)
+        groups(q + 1, *two)
         return 0
 
-    lax.fori_loop(0, NODES, node_loop, 0)
-
+    lax.fori_loop(0, (all_blocks + 1) >> 1, blocks_of_two, 0)
+
+    r = iota((width, 128), 0) & 15
     for j in range(width // 32):
         parts = [acc[k, 2 * j + half, 8 * w:8 * w + 8, :] for half in range(2) for w in range(2) for k in range(NODES)]
         t = jnp.concatenate(parts, axis=0).T
+        t = t - jnp.where(r == 0, 0.0, pltpu.roll(t, 1, 0))
+        t = t - jnp.where(r == 15, 0.0, pltpu.roll(t, width - 1, 0))
         for z in range(8):
             for c in range(2):
                 main_z[c, z, j] = t[(2 * z + c) * 16:(2 * z + c) * 16 + 8]
@@ -256,11 +259,13 @@
     ext[...] = jnp.concatenate(lines_ex, axis=0).T
     even, odd = ext[pl.ds(0, width // 2, stride=2), :], ext[pl.ds(1, width // 2, stride=2), :]
     both = even + pltpu.roll(odd, 16, 1)
-    for j in range(8):
+    for j2 in range(2):
+        packed = both[64 * j2:64 * j2 + 16]
+        for i in range(1, 4):
+            packed = packed + pltpu.roll(both[64 * j2 + 16 * i:64 * j2 + 16 * i + 16], 32 * i, 1)
         for z in range(8):
             for c in range(2):
-                p = j * 16 + z * 2 + c
-                extra[c, z, j] = both[p:p + 1]
+                extra[c, z, j2:j2 + 1] = packed[2 * z + c:2 * z + c + 1]
 
 
 def local_histogram(kept_count, features, kept_index, gh, node_ids, sample_flags):
@@ -273,16 +278,18 @@
         out_shape=(
             jax.ShapeDtypeStruct((2, 8, 8, 8, 128), F32),
             jax.ShapeDtypeStruct((2, 8, 8, 8, 128), F32),
-            jax.ShapeDtypeStruct((2, 8, 8, 1, 128), F32),
+            jax.ShapeDtypeStruct((2, 8, 2, 128), F32),
         ),
-        in_specs=[SM, HBM, VM, VM, VM, VM],
+        in_specs=[SM, VM, VM, VM, VM, VM],
         out_specs=(VM, VM, VM),
         scratch_shapes=[
-            pltpu.VMEM((rows, width), BF16),
             pltpu.VMEM((room, width), F32),
             pltpu.VMEM((room, 128), F32),
             pltpu.VMEM((NODES, lines, 128), F32),
             pltpu.VMEM((128, 128), BF16),
+            pltpu.VMEM((width, BLOCK), F32),
+            pltpu.VMEM((width, BLOCK), F32),
+            pltpu.VMEM((16, BLOCK), BF16),
             pltpu.VMEM((width, BLOCK), F32),
             pltpu.VMEM((width, BLOCK), F32),
             pltpu.VMEM((16, BLOCK), BF16),
@@ -292,10 +299,9 @@
             pltpu.VMEM((8, 128), I32),
             pltpu.SMEM((8, 128), I32),
             pltpu.VMEM((width, 128), F32),
-            pltpu.SemaphoreType.DMA((8,)),
             pltpu.SemaphoreType.DMA,
         ],
-        compiler_params=pltpu.CompilerParams(vmem_limit_bytes=56 << 20),
+        compiler_params=pltpu.CompilerParams(vmem_limit_bytes=30 << 20),
         name="local_histogram",
     )(
         kept_count,
@@ -308,11 +314,12 @@
 
 
 FAR_FIRST = (4, 3, 5, 2, 6, 1, 7)
+STEPS = 32000.0
 
 
 def reduce_body(
     main_z, main_y, extra, edges, out,
-    cz, cy, ce, sz, sy, se, rz, ry, re, uz, uy, ue, vz, vy, ve,
+    cz, cy, ce, qz, qy, fz, fy, rz, ry, gz, gy, uz, uy, ue, vz, vy, ve,
     sem1, sem2, sem3,
 ):
     row, feat = lax.axis_index("rows"), lax.axis_index("feat")
@@ -348,32 +355,48 @@
         for c in pair[d]:
             c.start()
 
+    def coded(v):
+        v = v.reshape(64, 128)
+        top = jnp.max(jnp.abs(v), axis=0, keepdims=True)
+        q = jnp.floor(v * jnp.where(top > 0.0, STEPS / top, 0.0) + 0.5)
+        return q.astype(I32).astype(jnp.int16), top * (1.0 / STEPS)
+
+    def plain(q, step):
+        return (q.astype(I32).astype(F32) * step).reshape(8, 8, 128)
+
     first = {}
     for d in FAR_FIRST + (0,):
         zz, yy = lax.rem(z + d, 8), lax.rem(y + d, 8)
         for c in pair[d]:
             c.wait_recv()
-        sz[zz] = main_z[core, zz] + cz[zz]
-        sy[yy] = main_y[core, yy] + cy[yy]
-        se[zz] = extra[core, zz] + ce[zz]
+        sz = main_z[core, zz] + cz[zz]
+        sy = main_y[core, yy] + cy[yy]
+        se = extra[core, zz] + ce[zz]
         if d:
+            qz[d - 1], step = coded(sz)
+            fz[d - 1, 0:2] = se
+            fz[d - 1, 2:3] = step
+            qy[d - 1], step = coded(sy)
+            fy[d - 1] = step
             first[d] = (
-                copy(sz.at[zz], rz.at[d - 1], sem2, d - 1, 0, to_z[d]),
-                copy(sy.at[yy], ry.at[d - 1], sem2, d - 1, 1, to_y[d]),
-                copy(se.at[zz], re.at[d - 1], sem2, d - 1, 2, to_z[d]),
+                copy(qz.at[d - 1], rz.at[d - 1], sem2, d - 1, 0, to_z[d]),
+                copy(qy.at[d - 1], ry.at[d - 1], sem2, d - 1, 1, to_y[d]),
+                copy(fz.at[d - 1], gz.at[d - 1], sem2, d - 1, 2, to_z[d]),
+                copy(fy.at[d - 1], gy.at[d - 1], sem2, d - 1, 3, to_y[d]),
             )
             for c in first[d]:
                 c.start()
-    az, ay, ae = sz[z], sy[y], se[z]
+    az, ay, ae = sz, sy, se
     for d in FAR_FIRST[::-1]:
         for c in first[d]:
             c.wait_recv()
-        az += rz[d - 1]
-        ay += ry[d - 1]
-        ae += re[d - 1]
+        az += plain(rz[d - 1], gz[d - 1, 2:3])
+        ay += plain(ry[d - 1], gy[d - 1])
+        ae += gz[d - 1, 0:2]
     uz[...] = az
     uy[...] = ay
-    ue[...] = ae
+    ue[0] = ae[0:1]
+    ue[1] = ae[1:2]
 
     second = {}
     for d in FAR_FIRST:
@@ -381,11 +404,11 @@
         second[d] = (
             copy(uz.at[yy], vz.at[d - 1], sem3, d - 1, 0, to_y[d]),
             copy(uy.at[zz], vy.at[d - 1], sem3, d - 1, 1, to_z[d]),
-            copy(ue.at[yy], ve.at[d - 1], sem3, d - 1, 2, to_y[d]),
+            copy(ue.at[yy // 4], ve.at[d - 1], sem3, d - 1, 2, to_y[d]),
         )
         for c in second[d]:
             c.start()
-    a, b, e = uz[y], uy[z], ue[y]
+    a, b, e = uz[y], uy[z], ue[y // 4]
     for d in FAR_FIRST[::-1]:
         for c in second[d]:
             c.wait_recv()
@@ -394,35 +417,40 @@
         e += ve[d - 1]
     out[pl.ds(0, 8), :] = a
     out[pl.ds(8, 8), :] = b
-    out[pl.ds(16, 1), :] = e
+    own = lax.rem(y, 4)
+    for i in range(4):
+
+        @pl.when(own == i)
+        def _():
+            out[pl.ds(16, 1), :] = pltpu.roll(jnp.broadcast_to(e, (8, 128)), (128 - 32 * i) % 128, 1)[0:1]
+
     out[pl.ds(17, 2), :] = edges[pl.ds(2 * row, 2), :].astype(F32)
     for c in [c for group in (pair, first, second) for some in group.values() for c in some]:
         c.wait_send()
 
 
 def reduce_rows(main_z, main_y, extra, cut_edges):
-    big, small = (8, 8, 8, 128), (8, 8, 1, 128)
+    big, small = (8, 8, 8, 128), (8, 2, 128)
+    coded = [pltpu.VMEM((7, 64, 128), jnp.int16)] * 2 + [pltpu.VMEM((7, 4, 128), F32), pltpu.VMEM((7, 1, 128), F32)]
     return pl.pallas_call(
         reduce_body,
         out_shape=jax.ShapeDtypeStruct((24, 128), F32),
         in_specs=[VM] * 4,
         out_specs=VM,
-        scratch_shapes=[pltpu.VMEM(s, F32) for s in (big, big, small, big, big, small)]
-        + [pltpu.VMEM((7,) + s[1:], F32) for s in (big, big, small)]
-        + [pltpu.VMEM(s[1:], F32) for s in (big, big, small)]
-        + [pltpu.VMEM((7,) + s[2:], F32) for s in (big, big, small)]
-        + [pltpu.SemaphoreType.DMA((2, n, 3)) for n in (8, 7, 7)],
-        compiler_params=pltpu.CompilerParams(collective_id=1, has_side_effects=True),
+        scratch_shapes=[pltpu.VMEM(s, F32) for s in (big, big, small)]
+        + coded
+        + coded
+        + [pltpu.VMEM(s, F32) for s in (big[1:], big[1:], (2, 1, 128))]
+        + [pltpu.VMEM(s, F32) for s in ((7, 8, 128), (7, 8, 128), (7, 1, 128))]
+        + [pltpu.SemaphoreType.DMA((2, n, m)) for n, m in ((8, 3), (7, 4), (7, 3))],
+        compiler_params=pltpu.CompilerParams(collective_id=1, has_side_effects=True, vmem_limit_bytes=12 << 20),
         name="reduce_rows",
     )(main_z, main_y, extra, cut_edges)
 
 
 def gain_body(sums, gain, rank):
-    a = sums[pl.ds(0, 16), :]
+    bins = sums[pl.ds(0, 16), :]
     b = sums[pl.ds(16, 1), :]
-    line = iota((16, 128), 0)
-    rest = a - jnp.where(line == 0, 0.0, pltpu.roll(a, 1, 0))
-    bins = rest - jnp.where(line == 15, 0.0, pltpu.roll(rest, 15, 0))
     hi = iota((16, 128), 1) & 7
     spread = jnp.concatenate([jnp.where(hi == h, bins, 0.0) for h in range(8)], axis=0)
     table = jnp.sum(spread.T.reshape(16, 8, 128), axis=1)
@@ -443,7 +471,7 @@
 
 def gains(sums):
     out = jax.ShapeDtypeStruct((2, NODES, 128), F32)
-    return pl.pallas_call(gain_body, out_shape=(out, out), in_specs=[VM], out_specs=(VM, VM), name="gains")(sums)
+    return pl.pallas_call(gain_body, out_shape=(out, out), in_specs=[VM], out_specs=(VM, VM), name="gains", compiler_params=pltpu.CompilerParams(vmem_limit_bytes=4 << 20))(sums)
 
 
 def shards(features, gradients, hessians, node_ids, sample_flags, kept_index, kept_count, cut_edges):

time: 64.5 us -> 55.6 us (0.86)
  Pallas kernels: 62.6 us -> 52 us
  local copies, waits for them, and re-layouts: 0 us -> 1.41 us
    pallas_call x1, Pallas kernels: 41.5 us -> 35.5 us  [reduce_rows(): pl.pallas_call(reduce_body, out_shape=jax.ShapeDtypeStruct((24, 128), F32...]
    pallas_call x1, Pallas kernels: 11.5 us -> 8.82 us  [local_histogram(): pl.pallas_call(hist_body, out_shape=(jax.ShapeDtypeStruct((2, 8, 8, 8, 12...]
    unnamed x0 -> x14, local copies, waits for them, and re-layouts: none -> 1.41 us
    pallas_call x1, Pallas kernels: 7.95 us -> 6.81 us  [share(): pl.pallas_call(functools.partial(share_body, peers), out_shape=jax.ShapeD...]
    pallas_call x1, Pallas kernels: 1.63 us -> 0.92 us  [gains(): pl.pallas_call(gain_body, out_shape=(out, out), in_specs=[VM], out_specs=...]
where the time goes in v3:
time: 55.6 us; the launch traced here: 54.8 us
  Pallas kernels  52 us (94%)
  local copies, waits for them, and re-layouts  1.41 us (3%)
  between operations  1.36 us (2%)
    pallas_call x1, Pallas kernels, reduce_rows(): pl.pallas_call(reduce_body, out_shape=jax.ShapeDtypeStruct((24, 128), F32...  35.5 us
    pallas_call x1, Pallas kernels, local_histogram(): pl.pallas_call(hist_body, out_shape=(jax.ShapeDtypeStruct((2, 8, 8, 8, 12...  8.82 us
    pallas_call x1, Pallas kernels, share(): pl.pallas_call(functools.partial(share_body, peers), out_shape=jax.ShapeD...  6.81 us
    unnamed x14, local copies, waits for them, and re-layouts  1.41 us

profile of v3, /device:TPU:1, one launch (start us, length us, event | category | flops | bytes accessed | tf_op | source)
XLA Modules:
  0.0 54.8 jit_solution(4490137629681173611)
XLA Ops:
  1.3 0.0 copy-start.5
  1.3 0.7 %copy-done.5 = f32[2048]{0:T(1024)S(1)} copy-done((f32[2048]{0:T(1024)S(1)}, f32[2048]{0:T(1024)}, u32[]{:S(2)}) %copy-start.5) | copy-done | bytes 8216
  2.0 0.0 copy-start.6
  2.0 0.7 %copy-done.6 = f32[2048]{0:T(1024)S(1)} copy-done((f32[2048]{0:T(1024)S(1)}, f32[2048]{0:T(1024)}, u32[]{:S(2)}) %copy-start.6) | copy-done | bytes 8216
  2.7 0.0 copy-start
  2.7 0.0 copy-start.2
  2.7 0.0 copy-start.3
  2.7 0.0 copy-start.4
  2.7 6.8 %share.1.gh = f32[4,2,16,128]{3,2,1,0:T(8,128)S(1)} custom-call(f32[16,128]{1,0:T(8,128)S(1)} %bitcast.8, f32[16,128]{1,0:T(8,128)S(1)} %bitcast.9), custom_call_target="tpu_custom_call" | custom-call | flops 5000000000 | bytes 8000000 | tf_op jit(solution)/shard_map/share/pallas_call | solution.py:57
  9.5 0.0 copy-done
  9.5 0.0 copy-done.2
  9.5 0.0 copy-done.3
  9.5 0.0 copy-done.4
  9.5 0.0 copy-start.1
  9.6 8.8 %local_histogram.1 = (f32[2,8,8,8,128]{4,3,2,1,0:T(8,128)S(1)}, f32[2,8,8,8,128]{4,3,2,1,0:T(8,128)S(1)}, f32[2,8,2,128]{3,2,1,0:T(2,128)S(1)}) custom-call(s32[1]{0:T(128)S(6)} %copy.10.cnt_s, bf16[8192,256]{1,0:T(8,128)(2,1)S(1)} %copy-done, s32[1,4096]{1,0:T(1,128)S(1)} %bitcast.7, f32[4,2,16,128]{3,2,1,0:T(8,128)S(1)} %share.1.gh, ...), custom_call_target="tpu_custom_call" | custom-call | tf_op jit(solution)/shard_map/local_histogram/pallas_call | solution.py:276
  18.4 0.0 copy-done.1
  18.4 35.5 %reduce_rows.1.sums = f32[24,128]{1,0:T(8,128)S(1)} custom-call(f32[2,8,8,8,128]{4,3,2,1,0:T(8,128)S(1)} %get-tuple-element.5.main_z, f32[2,8,8,8,128]{4,3,2,1,0:T(8,128)S(1)} %get-tuple-element.6.main_y, f32[2,8,2,128]{3,2,1,0:T(2,128)S(1)} %get-tuple-element.7.extra, s32[256,128]{1,0:T(8,128)S(1)} %copy-done.1), custom_call_target="tpu_custom_call" | custom-call | tf_op jit(solution)/shard_map/reduce_rows/pallas_call | solution.py:435
  53.8 0.9 %gains.1 = (f32[2,4,128]{2,1,0:T(4,128)}, f32[2,4,128]{2,1,0:T(4,128)}) custom-call(f32[24,128]{1,0:T(8,128)S(1)} %reduce_rows.1.sums), custom_call_target="tpu_custom_call" | custom-call | tf_op jit(solution)/shard_map/gains/pallas_call | solution.py:474
Async XLA Ops:
  1.3 0.7 %copy-start.5 = (f32[2048]{0:T(1024)S(1)}, f32[2048]{0:T(1024)}, u32[]{:S(2)}) copy-start(f32[2048]{0:T(1024)} %param.9) | copy-start | bytes 24580
  2.0 0.7 %copy-start.6 = (f32[2048]{0:T(1024)S(1)}, f32[2048]{0:T(1024)}, u32[]{:S(2)}) copy-start(f32[2048]{0:T(1024)} %param.10) | copy-start | bytes 24580
  2.7 6.8 %copy-start = (bf16[8192,256]{1,0:T(8,128)(2,1)S(1)}, bf16[8192,256]{1,0:T(8,128)(2,1)}, u32[]{:S(2)}) copy-start(bf16[8192,256]{1,0:T(8,128)(2,1)} %feat.1) | copy-start | bytes 12582916
  2.7 6.8 %copy-start.2 = (s32[8192]{0:T(1024)S(1)}, s32[8192]{0:T(1024)}, u32[]{:S(2)}) copy-start(s32[8192]{0:T(1024)} %param.11) | copy-start | bytes 98308
  2.7 6.8 %copy-start.3 = (s32[8192]{0:T(1024)S(1)}, s32[8192]{0:T(1024)}, u32[]{:S(2)}) copy-start(s32[8192]{0:T(1024)} %param.12) | copy-start | bytes 98308
  2.7 6.9 %copy-start.4 = (s32[4096]{0:T(1024)S(1)}, s32[4096]{0:T(1024)}, u32[]{:S(2)}) copy-start(s32[4096]{0:T(1024)} %param.13) | copy-start | bytes 49156
  9.5 8.8 %copy-start.1 = (s32[256,128]{1,0:T(8,128)S(1)}, s32[256,128]{1,0:T(8,128)}, u32[]{:S(2)}) copy-start(s32[256,128]{1,0:T(8,128)} %edges.1) | copy-start | bytes 393220

commit v4 on v3

--- a/solution.py
+++ b/solution.py
@@ -14,7 +14,6 @@
 NT = (((1,), (1,)), ((), ()))
 VM = pl.BlockSpec(memory_space=pltpu.VMEM)
 SM = pl.BlockSpec(memory_space=pltpu.SMEM)
-HBM = pl.BlockSpec(memory_space=pl.ANY)
 F32, BF16, I32 = jnp.float32, jnp.bfloat16, jnp.int32
 
 
@@ -26,12 +25,21 @@
     return jnp.where(cond, 1.0, 0.0).astype(BF16)
 
 
-def share_body(peers, g_ref, h_ref, out_ref, send_sem, recv_sem, own_sem):
+def share_body(
+    peers, cnt_s, g_ref, h_ref, idx_ref, node_ref, out_ref, ranks, offs, idx_v, node_v, send_sem, recv_sem, own_sem
+):
     row, me = lax.axis_index("rows"), lax.axis_index("feat")
+    lines = node_v.shape[0]
+    slots = idx_v.shape[1]
     barrier = pltpu.get_barrier_semaphore()
     for d in range(1, peers):
         pl.semaphore_signal(barrier, inc=1, device_id=(row, lax.rem(me + d, peers)), device_id_type=MESH)
     copies = [pltpu.make_async_copy(ref, out_ref.at[me, w], own_sem.at[w]) for w, ref in enumerate((g_ref, h_ref))]
+    fetch_idx = pltpu.make_async_copy(idx_ref, idx_v, own_sem.at[2])
+    fetch_node = pltpu.make_async_copy(node_ref, node_v, own_sem.at[3])
+    fetch_idx.start()
+    fetch_node.start()
+    count = cnt_s[0]
     pl.semaphore_wait(barrier, peers - 1)
     for d in range(1, peers):
         to = (row, lax.rem(me + d, peers))
@@ -48,33 +56,10 @@
             )
     for c in copies:
         c.start()
-    for c in copies:
-        c.wait()
-
-
-def share(gradients, hessians, peers):
-    part = gradients.shape[0]
-    return pl.pallas_call(
-        functools.partial(share_body, peers),
-        out_shape=jax.ShapeDtypeStruct((peers, 2, part // 128, 128), F32),
-        in_specs=[pl.BlockSpec(memory_space=pltpu.HBM)] * 2,
-        out_specs=VM,
-        scratch_shapes=[pltpu.SemaphoreType.DMA(n) for n in ((peers, 2), (peers, 2), (2,))],
-        compiler_params=pltpu.CompilerParams(collective_id=0, has_side_effects=True, vmem_limit_bytes=4 << 20),
-        cost_estimate=pl.CostEstimate(flops=5_000_000_000, bytes_accessed=8_000_000, transcendentals=0),
-        name="share",
-    )(gradients.reshape(part // 128, 128), hessians.reshape(part // 128, 128))
-
-
-def hist_body(
-    cnt_s, feat, idx_v, gh, node_v, flag_v, main_z, main_y, extra,
-    xs, ws, pos, tpose, hi_a, lo_a, w16_a, hi_b, lo_b, w16_b, acc, exacc, totacc, offs_v, offs_s, ext, osem,
-):
-    rows, width = feat.shape
-    lines = rows // 128
-    slots = idx_v.shape[1]
-    count = cnt_s[0]
-
+
+    fetch_idx.wait()
+    fetch_node.wait()
+    node = node_v[...]
     kept = jnp.zeros((lines, 128), F32)
     for q in range(slots // 1024):
         ids = idx_v[:, pl.ds(q * 1024, 1024)]
@@ -86,17 +71,48 @@
     before = onehot(iota((128, 128), 0) < iota((128, 128), 1))
     above = onehot(iota((lines, lines), 1) < iota((lines, lines), 0))
     upto = onehot(iota((lines, 128), 0) < iota((lines, 128), 1))
-    ranks = []
     for k in range(NODES):
-        mine = (kept > 0.5) & (node_v[...] == k)
+        mine = (kept > 0.5) & (node == k)
         ones = onehot(mine)
         per_line = jnp.sum(jnp.where(mine, 1.0, 0.0), axis=1, keepdims=True)
         rank = jnp.dot(ones, before, preferred_element_type=F32)
         rank += jnp.dot(above, jnp.broadcast_to(per_line, (lines, 128)).astype(BF16), preferred_element_type=F32)
-        ranks.append((mine, rank))
+        ranks[k] = jnp.where(mine, rank, -1.0)
         counts = lax.dot_general(jnp.ones((8, 128), BF16), ones, NT, preferred_element_type=F32)
         starts = jnp.dot(counts.astype(BF16), upto, preferred_element_type=F32)
-        offs_v[pl.ds(k, 1), :] = starts[0:1].astype(I32)
+        offs[pl.ds(k, 1), :] = starts[0:1].astype(I32)
+
+    for c in copies:
+        c.wait()
+
+
+def share(kept_count, gradients, hessians, kept_index, node_ids, peers):
+    part, slots, lines = gradients.shape[0], kept_index.shape[0], node_ids.shape[0] // 128
+    hbm = pl.BlockSpec(memory_space=pltpu.HBM)
+    big = [gradients.reshape(part // 128, 128), hessians.reshape(part // 128, 128), kept_index.reshape(1, slots), node_ids.reshape(lines, 128)]
+    return pl.pallas_call(
+        functools.partial(share_body, peers),
+        out_shape=(
+            jax.ShapeDtypeStruct((peers, 2, part // 128, 128), F32),
+            jax.ShapeDtypeStruct((NODES, lines, 128), F32),
+            jax.ShapeDtypeStruct((8, 128), I32),
+        ),
+        in_specs=[SM] + [hbm] * 4,
+        out_specs=(VM, VM, VM),
+        scratch_shapes=[pltpu.VMEM((1, slots), I32), pltpu.VMEM((lines, 128), I32)]
+        + [pltpu.SemaphoreType.DMA(n) for n in ((peers, 2), (peers, 2), (4,))],
+        compiler_params=pltpu.CompilerParams(collective_id=0, has_side_effects=True, vmem_limit_bytes=4 << 20),
+        cost_estimate=pl.CostEstimate(flops=5_000_000_000, bytes_accessed=8_000_000, transcendentals=0),
+        name="share",
+    )(kept_count, *[pltpu.with_memory_space_constraint(v, pltpu.HBM) for v in big])
+
+
+def hist_body(
+    feat, gh, ranks, offs_v, flag_v, main_z, main_y, extra,
+    xs, ws, pos, tpose, hi_a, lo_a, w16_a, hi_b, lo_b, w16_b, acc, exacc, totacc, offs_s, ext, osem,
+):
+    rows, width = feat.shape
+    lines = rows // 128
     to_scalar = pltpu.make_async_copy(offs_v, offs_s, osem)
     to_scalar.start()
 
@@ -123,8 +139,8 @@
         bases.append(base)
         blocks.append((sizes[k] + (BLOCK - 1)) // BLOCK)
         base = base + blocks[k] * BLOCK
-        mine, rank = ranks[k]
-        pos[k] = jnp.where(mine, rank + bases[k].astype(F32), -1.0)
+        rank = ranks[k]
+        pos[k] = jnp.where(rank >= 0.0, rank + bases[k].astype(F32), -1.0)
 
     place = iota((WIN, 256), 0).astype(F32).astype(BF16)
     lane = iota((128, 128), 1) & (lines - 1)
@@ -268,9 +284,8 @@
                 extra[c, z, j2:j2 + 1] = packed[2 * z + c:2 * z + c + 1]
 
 
-def local_histogram(kept_count, features, kept_index, gh, node_ids, sample_flags):
+def local_histogram(features, gh, ranks, offs, sample_flags, slots):
     rows, width = features.shape
-    slots = kept_index.shape[0]
     lines = rows // 128
     room = slots + NODES * BLOCK + 512
     return pl.pallas_call(
@@ -280,7 +295,7 @@
             jax.ShapeDtypeStruct((2, 8, 8, 8, 128), F32),
             jax.ShapeDtypeStruct((2, 8, 2, 128), F32),
         ),
-        in_specs=[SM, VM, VM, VM, VM, VM],
+        in_specs=[VM] * 5,
         out_specs=(VM, VM, VM),
         scratch_shapes=[
             pltpu.VMEM((room, width), F32),
@@ -296,7 +311,6 @@
             pltpu.VMEM((NODES, width // 16, 16, 256), F32),
             pltpu.VMEM((NODES, 16, width), F32),
             pltpu.VMEM((NODES, 16, BLOCK), F32),
-            pltpu.VMEM((8, 128), I32),
             pltpu.SMEM((8, 128), I32),
             pltpu.VMEM((width, 128), F32),
             pltpu.SemaphoreType.DMA,
@@ -304,11 +318,10 @@
         compiler_params=pltpu.CompilerParams(vmem_limit_bytes=30 << 20),
         name="local_histogram",
     )(
-        kept_count,
         features,
-        kept_index.reshape(1, slots),
         gh,
-        node_ids.reshape(lines, 128),
+        ranks,
+        offs,
         sample_flags.reshape(lines, 128),
     )
 
@@ -475,8 +488,8 @@
 
 
 def shards(features, gradients, hessians, node_ids, sample_flags, kept_index, kept_count, cut_edges):
-    gh = share(gradients, hessians, lax.axis_size("feat"))
-    main_z, main_y, extra = local_histogram(kept_count, features, kept_index, gh, node_ids, sample_flags)
+    gh, ranks, offs = share(kept_count, gradients, hessians, kept_index, node_ids, lax.axis_size("feat"))
+    main_z, main_y, extra = local_histogram(features, gh, ranks, offs, sample_flags, kept_index.shape[0])
     return gains(reduce_rows(main_z, main_y, extra, cut_edges))
 
 

time: 55.6 us -> 51.4 us (0.924); the launches traced: 54.8 us -> 51.2 us
  Pallas kernels: 52 us -> 49.9 us
  local copies, waits for them, and re-layouts: 1.41 us -> 0.01 us
    unnamed x14 -> x6, local copies, waits for them, and re-layouts: 1.41 us -> 0.01 us
    pallas_call x1, Pallas kernels: 8.82 us -> 7.61 us  [local_histogram(): pl.pallas_call(hist_body, out_shape=(jax.ShapeDtypeStruct((2, 8, 8, 8, 12...]
    pallas_call x1, Pallas kernels: 35.5 us -> 34.3 us  [reduce_rows(): pl.pallas_call(reduce_body, out_shape=jax.ShapeDtypeStruct((24, 128), F32...]
where the time goes in v4:
time: 51.4 us; the launch traced here: 51.2 us
  Pallas kernels  49.9 us (97%)
  between operations  1.35 us (3%)
    pallas_call x1, Pallas kernels, reduce_rows(): pl.pallas_call(reduce_body, out_shape=jax.ShapeDtypeStruct((24, 128), F32...  34.3 us
    pallas_call x1, Pallas kernels, local_histogram(): pl.pallas_call(hist_body, out_shape=(jax.ShapeDtypeStruct((2, 8, 8, 8, 12...  7.61 us
    pallas_call x1, Pallas kernels, share(): pl.pallas_call(functools.partial(share_body, peers), out_shape=(jax.Shape...  7.07 us

profile of v4, /device:TPU:1, one launch (start us, length us, event | category | flops | bytes accessed | tf_op | source)
XLA Modules:
  0.0 51.2 jit_solution(8064117680605205765)
XLA Ops:
  1.3 0.0 copy-start
  1.3 0.0 copy-start.2
  1.3 7.1 %share.1 = (f32[4,2,16,128]{3,2,1,0:T(8,128)S(1)}, f32[4,64,128]{2,1,0:T(8,128)S(1)}, s32[8,128]{1,0:T(8,128)S(1)}) custom-call(s32[1]{0:T(128)S(6)} %copy.10.cnt_s, f32[16,128]{1,0:T(8,128)} %bitcast.8, f32[16,128]{1,0:T(8,128)} %bitcast.9, s32[1,4096]{1,0:T(1,128)} %bitcast.7, s32[64,128]{1,0:T(8,128)} %bitcast.6), custom_call_target="tpu_custom_call" | custom-call | flops 5000000000 | bytes 8000000 | tf_op jit(solution)/shard_map/share/pallas_call | solution.py:93
  8.4 0.0 copy-start.1
  8.4 0.0 copy-done
  8.4 0.0 copy-done.2
  8.4 7.6 %local_histogram.1 = (f32[2,8,8,8,128]{4,3,2,1,0:T(8,128)S(1)}, f32[2,8,8,8,128]{4,3,2,1,0:T(8,128)S(1)}, f32[2,8,2,128]{3,2,1,0:T(2,128)S(1)}) custom-call(bf16[8192,256]{1,0:T(8,128)(2,1)S(1)} %copy-done, f32[4,2,16,128]{3,2,1,0:T(8,128)S(1)} %get-tuple-element.8.gh, f32[4,64,128]{2,1,0:T(8,128)S(1)} %get-tuple-element.9.ranks, ...), custom_call_target="tpu_custom_call" | custom-call | tf_op jit(solution)/shard_map/local_histogram/pallas_call | solution.py:291
  16.0 0.0 copy-done.1
  16.0 34.3 %reduce_rows.1.sums = f32[24,128]{1,0:T(8,128)S(1)} custom-call(f32[2,8,8,8,128]{4,3,2,1,0:T(8,128)S(1)} %get-tuple-element.11.main_z, f32[2,8,8,8,128]{4,3,2,1,0:T(8,128)S(1)} %get-tuple-element.12.main_y, f32[2,8,2,128]{3,2,1,0:T(2,128)S(1)} %get-tuple-element.13.extra, s32[256,128]{1,0:T(8,128)S(1)} %copy-done.1), custom_call_target="tpu_custom_call" | custom-call | tf_op jit(solution)/shard_map/reduce_rows/pallas_call | solution.py:448
  50.3 0.9 %gains.1 = (f32[2,4,128]{2,1,0:T(4,128)}, f32[2,4,128]{2,1,0:T(4,128)}) custom-call(f32[24,128]{1,0:T(8,128)S(1)} %reduce_rows.1.sums), custom_call_target="tpu_custom_call" | custom-call | tf_op jit(solution)/shard_map/gains/pallas_call | solution.py:487
Async XLA Ops:
  1.3 7.1 %copy-start = (bf16[8192,256]{1,0:T(8,128)(2,1)S(1)}, bf16[8192,256]{1,0:T(8,128)(2,1)}, u32[]{:S(2)}) copy-start(bf16[8192,256]{1,0:T(8,128)(2,1)} %feat.1) | copy-start | bytes 12582916
  1.3 7.1 %copy-start.2 = (s32[8192]{0:T(1024)S(1)}, s32[8192]{0:T(1024)}, u32[]{:S(2)}) copy-start(s32[8192]{0:T(1024)} %param.12) | copy-start | bytes 98308
  8.4 7.7 %copy-start.1 = (s32[256,128]{1,0:T(8,128)S(1)}, s32[256,128]{1,0:T(8,128)}, u32[]{:S(2)}) copy-start(s32[256,128]{1,0:T(8,128)} %edges.1) | copy-start | bytes 393220
